TPU v7x, 32 devices: a whole 2x2x4 slice. The times are simulated.
32 devices in a mesh: seq: 16 (over z, x, core), chan: 2 (over y).
Axes of the slice: x: 2, y: 2, z: 4, core: 2. Of those that a mesh axis runs over, the one named last changes fastest.
Arguments:
- inputs: bfloat16 [4096, 2048], P('chan', 'seq'), may hold values from -6 to 6
- gating: bfloat16 [4096, 2048], P('chan', 'seq'), may hold values from -6 to 6
- grad_out: bfloat16 [4096, 2048], P('chan', 'seq'), may hold values from -6 to 6
- filters: float32 [64, 2048], P(None, ('seq', 'chan')), as said below
Outputs:
- grad_inputs: bfloat16 [4096, 2048], P('chan', 'seq')
- grad_gating: bfloat16 [4096, 2048], P('chan', 'seq')
- grad_filters: float32 [64, 2048], P(None, ('seq', 'chan'))
Inputs may be any that keep to these rules, and one draw needn't show every extreme that they name: `filters`: every entry's magnitude is at most 0.77 times the square root of 131072.
All inputs are finite; a program needn't handle non-finite values.
Results may differ from a plain program's by a relative error of at most 0.0049.
Values may be sent and summed in bfloat16 or wider, within the bound.
A program may use at most 64 MiB of HBM per device.

v0:
```python
import functools
import math

import jax
import jax.numpy as jnp
from jax import lax
from jax.experimental import pallas as pl
from jax.experimental.pallas import tpu as pltpu
from jax.sharding import PartitionSpec as P

D = 4096
G = 64


HIGHEST = lax.Precision.HIGHEST


def make_tables(seq_count, block_len):
    outer = 2 * seq_count
    total = outer * block_len
    outer_index = jnp.arange(outer, dtype=jnp.int32)
    block_index = jnp.arange(seq_count, dtype=jnp.int32)
    inner_index = jnp.arange(block_len, dtype=jnp.int32)
    block_angle = (outer_index[:, None] * block_index[None, :] % outer).astype(jnp.float32) * (
        2.0 * math.pi / outer
    )
    twist_angle = (outer_index[:, None] * inner_index[None, :] % total).astype(jnp.float32) * (
        2.0 * math.pi / total
    )
    inner_angle = (inner_index[:, None] * inner_index[None, :] % block_len).astype(jnp.float32) * (
        2.0 * math.pi / block_len
    )
    return (
        jnp.cos(block_angle),
        jnp.sin(block_angle),
        jnp.cos(twist_angle),
        jnp.sin(twist_angle),
        jnp.cos(inner_angle),
        jnp.sin(inner_angle),
    )


def right_product(values, table):
    return jnp.einsum("ckm,mj->ckj", values, table, precision=HIGHEST)


def forward_dft(signal, tables):
    block_cos, block_sin, twist_cos, twist_sin, inner_cos, inner_sin = tables
    real_first = jnp.einsum("kn,cnm->ckm", block_cos, signal, precision=HIGHEST)
    imag_first = -jnp.einsum("kn,cnm->ckm", block_sin, signal, precision=HIGHEST)
    real_twist = real_first * twist_cos + imag_first * twist_sin
    imag_twist = imag_first * twist_cos - real_first * twist_sin
    real_spec = right_product(real_twist, inner_cos) + right_product(imag_twist, inner_sin)
    imag_spec = right_product(imag_twist, inner_cos) - right_product(real_twist, inner_sin)
    return (real_spec, imag_spec)


def inverse_dft(real_spec, imag_spec, tables):
    block_cos, block_sin, twist_cos, twist_sin, inner_cos, inner_sin = tables
    real_first = right_product(real_spec, inner_cos) - right_product(imag_spec, inner_sin)
    imag_first = right_product(real_spec, inner_sin) + right_product(imag_spec, inner_cos)
    real_twist = real_first * twist_cos - imag_first * twist_sin
    imag_twist = real_first * twist_sin + imag_first * twist_cos
    total = real_spec.shape[1] * real_spec.shape[2]
    result = jnp.einsum("kn,ckm->cnm", block_cos, real_twist, precision=HIGHEST)
    result = result - jnp.einsum("kn,ckm->cnm", block_sin, imag_twist, precision=HIGHEST)
    return result / total


def shards(inputs, gating, grad_out, filters):
    seq_count = lax.axis_size("seq")
    chan_count = lax.axis_size("chan")
    chan_rows, block_len = inputs.shape
    local_chan = chan_rows // seq_count
    group_width = D // G
    groups_here = G // chan_count
    local_groups = max(1, local_chan // group_width)
    group_share = local_chan // local_groups
    copies = max(1, seq_count // groups_here)
    length = block_len * seq_count
    outer = 2 * seq_count
    factor = 1.0 / math.sqrt(group_width * length)
    tables = make_tables(seq_count, block_len)
    whole = lax.all_gather(filters, ("seq", "chan"), axis=1, tiled=True)
    first_group = (
        lax.axis_index("chan") * chan_rows + lax.axis_index("seq") * local_chan
    ) // group_width
    kernel_rows = lax.dynamic_slice_in_dim(whole, first_group, local_groups, 0)
    kernel_blocks = kernel_rows.reshape(local_groups, seq_count, block_len)
    kernel_real, kernel_imag = forward_dft(kernel_blocks * factor, tables)
    kernel_real = kernel_real[:, None]
    kernel_imag = kernel_imag[:, None]
    shaped_inputs = inputs.reshape(chan_rows, 1, block_len)
    values, gate_part, upstream = (
        lax.all_to_all(shaped_inputs, "seq", split_axis=0, concat_axis=1, tiled=True),
        lax.all_to_all(
            gating.reshape(chan_rows, 1, block_len), "seq", split_axis=0, concat_axis=1, tiled=True
        ),
        lax.all_to_all(
            grad_out.reshape(chan_rows, 1, block_len),
            "seq",
            split_axis=0,
            concat_axis=1,
            tiled=True,
        ),
    )
    input_real, input_imag = forward_dft(values.astype(jnp.float32), tables)
    upstream_f = upstream.astype(jnp.float32)
    product_b = lax.optimization_barrier(
        (gate_part.astype(jnp.float32) * upstream_f).astype(jnp.bfloat16)
    )
    up_real, up_imag = forward_dft(product_b.astype(jnp.float32), tables)
    grouped_shape = (local_groups, group_share, outer, block_len)
    input_real = input_real.reshape(grouped_shape)
    input_imag = input_imag.reshape(grouped_shape)
    up_real = up_real.reshape(grouped_shape)
    up_imag = up_imag.reshape(grouped_shape)
    flat_shape = (local_chan, outer, block_len)
    conv_real = input_real * kernel_real - input_imag * kernel_imag
    conv_imag = input_real * kernel_imag + input_imag * kernel_real
    convolved = inverse_dft(conv_real.reshape(flat_shape), conv_imag.reshape(flat_shape), tables)
    conv_b = convolved.astype(jnp.bfloat16)
    second = (upstream_f * lax.optimization_barrier(conv_b).astype(jnp.float32)).astype(
        jnp.bfloat16
    )
    back_real = up_real * kernel_real + up_imag * kernel_imag
    back_imag = up_imag * kernel_real - up_real * kernel_imag
    grad_input = inverse_dft(
        back_real.reshape(flat_shape), back_imag.reshape(flat_shape), tables
    ).astype(jnp.bfloat16)
    returned_input, returned_second = (
        lax.all_to_all(grad_input, "seq", split_axis=1, concat_axis=0, tiled=True),
        lax.all_to_all(second, "seq", split_axis=1, concat_axis=0, tiled=True),
    )
    returned_second = returned_second.reshape(chan_rows, block_len)
    cross_real = jnp.sum(input_real * up_real + input_imag * up_imag, axis=1)
    cross_imag = jnp.sum(input_real * up_imag - input_imag * up_real, axis=1)
    partial_grad = inverse_dft(cross_real, cross_imag, tables) * factor
    received = lax.all_to_all(partial_grad, "seq", split_axis=1, concat_axis=0, tiled=True)
    summed = received.reshape(groups_here, copies, block_len).sum(axis=1)
    grad_filters = lax.all_to_all(summed, "chan", split_axis=1, concat_axis=0, tiled=True)
    return (returned_input.reshape(chan_rows, block_len), returned_second, grad_filters)


GROUP_WIDTH = D // G
MESH = pl.DeviceIdType.MESH
TILE = 256
LAYERS = 4
DELAY_B, DELAY_C, DELAY_D = 1, 2, 4


def layered_kernel(
    seq_count,
    chan_count,
    x_ref,
    gate_hbm,
    up_hbm,
    raw_ref,
    gi_ref,
    gg_ref,
    grad_ref,
    gate_ref,
    up_ref,
    filt_ref,
    gf_ref,
    u_loc,
    xs,
    us,
    ks,
    cv,
    gv,
    acc_c,
    acc_g,
    conv_in,
    fg_out,
    held,
    part_out,
    part_in,
    x_send,
    x_recv,
    u_send,
    u_recv,
    c_send,
    c_recv,
    g_send,
    g_recv,
    z_send,
    z_recv,
    p_send,
    p_recv,
    k_send,
    k_recv,
    f_send,
    f_recv,
    in_sem,
):
    seq = lax.axis_index("seq")
    chan = lax.axis_index("chan")
    peers = seq_count // LAYERS
    layer = seq // peers
    spot = lax.rem(seq, peers)
    last = LAYERS - 1
    everyone = seq_count * chan_count
    me = seq * chan_count + chan
    groups = xs.shape[0]
    block = x_ref.shape[1]
    per_tile = TILE // block
    length = block * seq_count
    tiles = length // TILE
    width = GROUP_WIDTH
    rows = tiles * width
    layer_rows = rows // LAYERS
    local_chan = groups * width

    barrier = pltpu.get_barrier_semaphore()

    def all_loop(body):
        def step(k, carry):
            body(lax.rem(me + k, everyone))
            return carry

        lax.fori_loop(1, everyone, step, 0)

    def peer_loop(body):
        for k in range(1, peers):
            body(lax.rem(spot + k, peers))

    def group_loop(body):
        def step(g, carry):
            body(g)
            return carry

        lax.fori_loop(0, groups, step, 0)

    def greet(p):
        pl.semaphore_signal(
            barrier,
            inc=1,
            device_id=(p // chan_count, lax.rem(p, chan_count)),
            device_id_type=MESH,
        )

    gate_in = pltpu.make_async_copy(gate_hbm, gate_ref, in_sem.at[0])
    up_in = pltpu.make_async_copy(up_hbm, up_ref, in_sem.at[1])
    gate_in.start()
    up_in.start()
    all_loop(greet)
    share = raw_ref.shape[1]
    factor = 1.0 / math.sqrt(width * length)
    scaled = raw_ref[...] * factor
    lanes = jnp.concatenate([scaled] * chan_count, axis=1)
    kept = lax.broadcasted_iota(jnp.int32, lanes.shape, 1) // share == chan
    lanes = jnp.where(kept, lanes, 0.0)
    for i in range(chan_count * peers):
        filt_ref[i] = lanes[i * groups : (i + 1) * groups, :]
    gate_in.wait()
    up_in.wait()
    u_loc[...] = (
        gate_ref[...].astype(jnp.float32) * up_ref[...].astype(jnp.float32)
    ).astype(jnp.bfloat16)
    fg_out[...] = jnp.zeros_like(fg_out)
    pl.semaphore_wait(barrier, everyone - 1)

    def place(ref, g, s):
        return ref.at[
            g,
            pl.ds(pl.multiple_of((s // per_tile) * width, width), width),
            pl.ds(pl.multiple_of(lax.rem(s, per_tile) * block, block), block),
        ]

    def strip(ref, q, g):
        return ref.at[pl.ds(pl.multiple_of(q * local_chan + g * width, width), width), :]

    def remote(src, dst, send, recv, to_seq, to_chan=None):
        return pltpu.make_async_remote_copy(
            src_ref=src,
            dst_ref=dst,
            send_sem=send,
            recv_sem=recv,
            device_id=(to_seq, chan if to_chan is None else to_chan),
            device_id_type=MESH,
        )

    def forward(ref, buf, send, recv, g, to, slot):
        return remote(
            strip(ref, to, g),
            place(buf, g, layer * peers + slot),
            send.at[g, to],
            recv.at[g, slot],
            layer * peers + to,
        )

    def own(ref, buf, recv, g):
        return pltpu.make_async_copy(strip(ref, spot, g), place(buf, g, seq), recv.at[g, spot])

    def backward(buf, ref, send, recv, g, to, slot):
        return remote(
            place(buf, g, to),
            strip(ref, slot, g),
            send.at[g, to],
            recv.at[g, slot],
            layer * peers + to,
        )

    def own_back(buf, ref, recv, g):
        return pltpu.make_async_copy(place(buf, g, spot), strip(ref, spot, g), recv.at[g, spot])

    def give_back(buf, ref, send, recv, g):
        peer_loop(lambda p: backward(buf, ref, send, recv, g, p, spot).start())
        own_back(buf, ref, recv, g).start()

    def take_back(buf, ref, send, recv, g):
        peer_loop(lambda p: backward(buf, ref, send, recv, g, spot, p).wait_recv())
        own_back(buf, ref, recv, g).wait()

    def hop(buf, g, which, step):
        ref = buf.at[g, pl.ds(which * layer_rows, layer_rows), :]
        to = jnp.clip(layer + step, 0, last) * peers + spot
        return remote(ref, ref, z_send.at[g, which], z_recv.at[g, which], to)

    def hand(g, step):
        to = jnp.clip(layer + step, 0, last) * peers + spot
        return remote(part_out.at[g], part_in.at[g], p_send.at[g], p_recv.at[g], to)

    def filt_copy(to, slot):
        to_seq, to_chan = to // chan_count, lax.rem(to, chan_count)
        return remote(
            filt_ref.at[to_chan * peers + lax.rem(to_seq, peers)],
            ks.at[slot],
            k_send.at[to],
            k_recv.at[slot],
            to_seq,
            to_chan,
        )

    def grad_copy(to, slot):
        to_seq, to_chan = to // chan_count, lax.rem(to, chan_count)
        from_seq, from_chan = slot // chan_count, lax.rem(slot, chan_count)
        return remote(
            fg_out.at[to_seq],
            gf_ref.at[from_chan * seq_count + from_seq],
            f_send.at[to],
            f_recv.at[slot],
            to_seq,
            to_chan,
        )

    def scatter(ref, buf, send, recv, g):
        peer_loop(lambda p: forward(ref, buf, send, recv, g, p, spot).start())
        own(ref, buf, recv, g).start()

    def scatter_both(g):
        scatter(x_ref, xs, x_send, x_recv, g)
        scatter(u_loc, us, u_send, u_recv, g)

    scatter_both(0)
    all_loop(lambda p: filt_copy(p, me).start())
    own_filt = pltpu.make_async_copy(filt_ref.at[chan * peers + spot], ks.at[me], k_recv.at[me])
    own_filt.start()

    def scatter_rest(g):
        @pl.when(g > 0)
        def _():
            scatter_both(g)

    group_loop(scatter_rest)

    for which in range(LAYERS):
        span = slice(which * layer_rows, (which + 1) * layer_rows)
        empty = jnp.zeros((groups, layer_rows, TILE), jnp.bfloat16)
        has_u = (layer == which) | ((layer < which) & (layer > 0))

        @pl.when(jnp.logical_not(has_u))
        def _():
            us[:, span, :] = empty

    us[:, rows:, :] = jnp.zeros((groups, rows, TILE), jnp.bfloat16)
    row_id = lax.broadcasted_iota(jnp.int32, (TILE, TILE), 0)
    col_id = lax.broadcasted_iota(jnp.int32, (TILE, TILE), 1)
    upper = col_id >= row_id
    flip = jnp.where(row_id + col_id == TILE - 1, 1.0, 0.0).astype(jnp.bfloat16)
    lower_flipped = col_id + row_id >= TILE - 1
    nt = (((1,), (1,)), ((), ()))
    nn = (((1,), (0,)), ((), ()))
    half = tiles // LAYERS

    def dot(a, b, dims):
        return lax.dot_general(a, b, dims, preferred_element_type=jnp.float32)

    def gather_layer(g):
        peer_loop(lambda p: forward(x_ref, xs, x_send, x_recv, g, spot, p).wait_recv())
        own(x_ref, xs, x_recv, g).wait()
        peer_loop(lambda p: forward(u_loc, us, u_send, u_recv, g, spot, p).wait_recv())
        own(u_loc, us, u_recv, g).wait()
        for which in (0, 1):

            @pl.when(layer == which)
            def _():
                hop(xs, g, which, 1).start()

        for which in (2, 3):

            @pl.when(layer == which)
            def _():
                hop(us, g, which, -1).start()

    def relay(g):
        @pl.when(layer == 1)
        def _():
            hop(xs, g, 0, 1).wait_recv()
            hop(xs, g, 0, 1).start()

        @pl.when(layer == 2)
        def _():
            hop(us, g, 3, -1).wait_recv()
            hop(us, g, 3, -1).start()

    def compute(g):
        @pl.when(g == 0)
        def _():
            all_loop(lambda p: filt_copy(me, p).wait_recv())
            own_filt.wait()

        for which in range(LAYERS):

            @pl.when(layer == which)
            def _(which=which):
                compute_for(which, g)

    def compute_for(which, g):
        low_end, high_end = which * half, (which + 1) * half - 1
        x_first = low_end if which == last else 0
        u_last = high_end if which == 0 else tiles - 1
        conv_last = tiles - 1 if which == 2 else high_end
        grad_first = 0 if which == 1 else low_end
        gram_first = 0 if which == 1 else low_end
        if which == 1:
            hop(us, g, 2, -1).wait_recv()
            hop(us, g, 3, -1).wait_recv()
        if which == 2:
            hop(xs, g, 1, 1).wait_recv()
            hop(xs, g, 0, 1).wait_recv()

        def span(first, final):
            return slice(first * width, (final + 1) * width)

        acc_c[span(low_end, conv_last), :] = jnp.zeros(
            ((conv_last - low_end + 1) * width, TILE), jnp.float32
        )
        acc_g[span(grad_first, high_end), :] = jnp.zeros(
            ((high_end - grad_first + 1) * width, TILE), jnp.float32
        )
        rolled_before = jnp.zeros((TILE, TILE), jnp.float32)
        for lag in range(tiles):
            first, final = max(x_first, low_end - lag), min(high_end, conv_last - lag)
            u_from, u_to = max(low_end, grad_first + lag), min(u_last, high_end + lag)
            if first > final and u_from > u_to:
                break
            pieces = []
            for q in range(per_tile):
                s = lag * per_tile + q
                part = ks[s * chan_count, pl.ds(g, 1), :]
                for c in range(1, chan_count):
                    part = part + ks[s * chan_count + c, pl.ds(g, 1), :]
                pieces.append(part)
            row = jnp.concatenate(pieces, axis=1)
            rolled = pltpu.roll(
                jnp.broadcast_to(row, (TILE, TILE)), 0, 1, stride=1, stride_axis=0
            )
            table = jnp.where(upper, rolled, rolled_before)
            rolled_before = rolled
            high = table.astype(jnp.bfloat16)
            low = (table - high.astype(jnp.float32)).astype(jnp.bfloat16)
            if first <= final:
                xin = xs[g, span(first, final), :]
                acc_c[span(first + lag, final + lag), :] += dot(xin, high, nn) + dot(xin, low, nn)
            if u_from <= u_to:
                uin = us[g, span(u_from, u_to), :]
                acc_g[span(u_from - lag, u_to - lag), :] += dot(uin, high, nt) + dot(uin, low, nt)

        mine = span(low_end, high_end)
        if which == 2:
            part_out[g] = acc_c[last * layer_rows :, :]
            hand(g, 1).start()
        if which == 1:
            part_out[g] = acc_g[:layer_rows, :]
            hand(g, -1).start()
        if which < last:
            cv[g] = acc_c[mine, :].astype(jnp.bfloat16)
            give_back(cv, conv_in, c_send, c_recv, g)
        else:
            held[g] = acc_c[mine, :]
        if which > 0:
            gv[g] = acc_g[mine, :].astype(jnp.bfloat16)
            give_back(gv, gi_ref, g_send, g_recv, g)
        else:
            held[g] = acc_g[mine, :]

        x_span = span(gram_first, high_end)
        x_rows = (high_end - gram_first + 1) * width
        turned = dot(flip, xs[g, x_span, :], nt).astype(jnp.bfloat16)

        def gram_of(lag):
            start = (gram_first + lag) * width
            return dot(turned, us[g, start : start + x_rows, :], nn)

        gram = gram_of(0)
        final_lag = u_last - gram_first
        for lag in range(final_lag + 1):
            following = gram_of(lag + 1) if lag < final_lag else jnp.zeros_like(gram)
            mixed = jnp.where(lower_flipped, gram, following)
            gram = following
            aligned = pltpu.roll(mixed, 1, 1, stride=1, stride_axis=0)
            total = jnp.sum(aligned, axis=0, keepdims=True) * factor
            for q in range(per_tile):
                fg_out[lag * per_tile + q, pl.ds(g, 1), :] = total[:, q * block : (q + 1) * block]

    def finish(g):
        @pl.when(layer == last)
        def _():
            hand(g, 1).wait_recv()
            cv[g] = (held[g] + part_in[g]).astype(jnp.bfloat16)
            give_back(cv, conv_in, c_send, c_recv, g)

        @pl.when(layer == 0)
        def _():
            hand(g, -1).wait_recv()
            gv[g] = (held[g] + part_in[g]).astype(jnp.bfloat16)
            give_back(gv, gi_ref, g_send, g_recv, g)

    def stage(step, delay, body):
        @pl.when((step >= delay) & (step < groups + delay))
        def _():
            body(step - delay)

    def pipeline(step, carry):
        stage(step, 0, gather_layer)
        stage(step, DELAY_B, relay)
        stage(step, DELAY_C, compute)
        stage(step, DELAY_D, finish)
        return carry

    lax.fori_loop(0, groups + DELAY_C, pipeline, 0)
    all_loop(lambda p: grad_copy(p, me).start())
    own_grad = pltpu.make_async_copy(
        fg_out.at[seq], gf_ref.at[chan * seq_count + seq], f_recv.at[me]
    )
    own_grad.start()
    for g in range(groups + DELAY_C - DELAY_D, groups):
        finish(g)

    group_loop(lambda g: take_back(cv, conv_in, c_send, c_recv, g))
    gg_ref[...] = (up_ref[...].astype(jnp.float32) * conv_in[...].astype(jnp.float32)).astype(
        jnp.bfloat16
    )
    group_loop(lambda g: take_back(gv, gi_ref, g_send, g_recv, g))
    all_loop(lambda p: grad_copy(me, p).wait_recv())
    own_grad.wait()
    for c in range(chan_count):
        for q in range(peers):
            total = gf_ref[c * seq_count + q]
            for which in range(1, LAYERS):
                total = total + gf_ref[c * seq_count + which * peers + q]
            kept_part = total[:, :share]
            for d in range(1, chan_count):
                kept_part = jnp.where(chan == d, total[:, d * share : (d + 1) * share], kept_part)
            at = (c * peers + q) * groups
            grad_ref[at : at + groups, :] = kept_part

    def drain(g):
        peer_loop(lambda p: forward(x_ref, xs, x_send, x_recv, g, p, spot).wait_send())
        peer_loop(lambda p: forward(u_loc, us, u_send, u_recv, g, p, spot).wait_send())
        peer_loop(lambda p: backward(cv, conv_in, c_send, c_recv, g, p, spot).wait_send())
        peer_loop(lambda p: backward(gv, gi_ref, g_send, g_recv, g, p, spot).wait_send())

        @pl.when(layer == 0)
        def _():
            hop(xs, g, 0, 1).wait_send()

        @pl.when(layer == 1)
        def _():
            hop(xs, g, 0, 1).wait_send()
            hop(xs, g, 1, 1).wait_send()
            hand(g, -1).wait_send()

        @pl.when(layer == 2)
        def _():
            hop(us, g, 2, -1).wait_send()
            hop(us, g, 3, -1).wait_send()
            hand(g, 1).wait_send()

        @pl.when(layer == 3)
        def _():
            hop(us, g, 3, -1).wait_send()

    group_loop(drain)
    all_loop(lambda p: filt_copy(p, me).wait_send())
    all_loop(lambda p: grad_copy(p, me).wait_send())


def layered_shards(inputs, gating, grad_out, filters):
    seq_count = lax.axis_size("seq")
    chan_count = lax.axis_size("chan")
    chan_rows, block = inputs.shape
    everyone = seq_count * chan_count
    peers = seq_count // LAYERS
    groups = chan_rows // peers // GROUP_WIDTH
    length = block * seq_count
    rows = length // TILE * GROUP_WIDTH
    layer_rows = rows // LAYERS
    vmem = pl.BlockSpec(memory_space=pltpu.VMEM)
    hbm = pl.BlockSpec(memory_space=pltpu.HBM)
    pair = pltpu.SemaphoreType.DMA((groups, peers))
    stacked = pltpu.SemaphoreType.DMA((groups, LAYERS))
    single = pltpu.SemaphoreType.DMA((groups,))
    many = pltpu.SemaphoreType.DMA((everyone,))
    return pl.pallas_call(
        functools.partial(layered_kernel, seq_count, chan_count),
        out_shape=(
            jax.ShapeDtypeStruct((chan_rows, block), jnp.bfloat16),
            jax.ShapeDtypeStruct((chan_rows, block), jnp.bfloat16),
            jax.ShapeDtypeStruct(filters.shape, jnp.float32),
        ),
        in_specs=[hbm, hbm, hbm, vmem],
        out_specs=(vmem, vmem, vmem),
        scratch_shapes=[
            pltpu.VMEM((chan_rows, block), jnp.bfloat16),
            pltpu.VMEM((chan_rows, block), jnp.bfloat16),
            pltpu.VMEM((chan_count * peers, groups, block), jnp.float32),
            pltpu.VMEM((everyone, groups, block), jnp.float32),
            pltpu.VMEM((chan_rows, block), jnp.bfloat16),
            pltpu.VMEM((groups, rows, TILE), jnp.bfloat16),
            pltpu.VMEM((groups, 2 * rows, TILE), jnp.bfloat16),
            pltpu.VMEM((everyone, groups, block), jnp.float32),
            pltpu.VMEM((groups, layer_rows, TILE), jnp.bfloat16),
            pltpu.VMEM((groups, layer_rows, TILE), jnp.bfloat16),
            pltpu.VMEM((rows, TILE), jnp.float32),
            pltpu.VMEM((rows, TILE), jnp.float32),
            pltpu.VMEM((chan_rows, block), jnp.bfloat16),
            pltpu.VMEM((seq_count, groups, block), jnp.float32),
            pltpu.VMEM((groups, layer_rows, TILE), jnp.float32),
            pltpu.VMEM((groups, layer_rows, TILE), jnp.float32),
            pltpu.VMEM((groups, layer_rows, TILE), jnp.float32),
        ]
        + [pair] * 8
        + [stacked] * 2
        + [single] * 2
        + [many] * 4
        + [pltpu.SemaphoreType.DMA((2,))],
        compiler_params=pltpu.CompilerParams(
            collective_id=0, has_side_effects=True, vmem_limit_bytes=40 * 1024 * 1024
        ),
    )(inputs, gating, grad_out, filters)


def solution(mesh):
    placed = (P("chan", "seq"), P("chan", "seq"), P("chan", "seq"), P(None, ("seq", "chan")))
    layered = mesh.shape["seq"] == 16 and mesh.shape["chan"] == 2
    return jax.shard_map(
        layered_shards if layered else shards,
        mesh=mesh,
        in_specs=placed,
        out_specs=(P("chan", "seq"), P("chan", "seq"), P(None, ("seq", "chan"))),
        check_vma=False,
    )
```

profile of v0, /device:TPU:0, one launch (start us, length us, event | category | flops | bytes accessed | tf_op | source)
XLA Modules:
  0.0 62.0 jit_solution(5145464958009732059)
XLA Ops:
  0.6 0.0 copy-start
  0.6 1.0 %copy-done = bf16[2048,128]{1,0:T(8,128)(2,1)S(1)} copy-done((bf16[2048,128]{1,0:T(8,128)(2,1)S(1)}, bf16[2048,128]{1,0:T(8,128)(2,1)}, u32[]{:S(2)}) %copy-start) | copy-done | bytes 524312
  1.7 0.0 copy-start.1
  1.7 1.0 %copy-done.1 = bf16[2048,128]{1,0:T(8,128)(2,1)S(1)} copy-done((bf16[2048,128]{1,0:T(8,128)(2,1)S(1)}, bf16[2048,128]{1,0:T(8,128)(2,1)}, u32[]{:S(2)}) %copy-start.1) | copy-done | bytes 524312
  2.7 0.0 copy-start.2
  2.7 1.0 %copy-done.2 = bf16[2048,128]{1,0:T(8,128)(2,1)S(1)} copy-done((bf16[2048,128]{1,0:T(8,128)(2,1)S(1)}, bf16[2048,128]{1,0:T(8,128)(2,1)}, u32[]{:S(2)}) %copy-start.2) | copy-done | bytes 524312
  3.8 0.0 copy-start.3
  3.8 0.8 %copy-done.3 = f32[64,64]{1,0:T(8,128)S(1)} copy-done((f32[64,64]{1,0:T(8,128)S(1)}, f32[64,64]{1,0:T(8,128)}, u32[]{:S(2)}) %copy-start.3) | copy-done | bytes 16408
  4.5 55.2 %shard_map.67 = (bf16[2048,128]{1,0:T(8,128)(2,1)S(1)}, bf16[2048,128]{1,0:T(8,128)(2,1)S(1)}, f32[64,64]{1,0:T(8,128)S(1)}) custom-call(bf16[2048,128]{1,0:T(8,128)(2,1)S(1)} %copy-done, bf16[2048,128]{1,0:T(8,128)(2,1)S(1)} %copy-done.1, bf16[2048,128]{1,0:T(8,128)(2,1)S(1)} %copy-done.2, f32[64,64]{1,0:T(8,128)S(1)} %copy-done.3), custom_call_target="tpu_custom_call" | custom-call | tf_op jit(solution)/shard_map/pallas_call | solution.py:617
  59.8 0.8 %copy.10 = bf16[2048,128]{1,0:T(8,128)(2,1)} copy(bf16[2048,128]{1,0:T(8,128)(2,1)S(1)} %get-tuple-element.6) | data formatting | bytes 1048576
  60.6 0.8 %copy.11 = bf16[2048,128]{1,0:T(8,128)(2,1)} copy(bf16[2048,128]{1,0:T(8,128)(2,1)S(1)} %get-tuple-element.7) | data formatting | bytes 1048576
  61.4 0.6 copy.12
Async XLA Ops:
  0.6 1.0 %copy-start = (bf16[2048,128]{1,0:T(8,128)(2,1)S(1)}, bf16[2048,128]{1,0:T(8,128)(2,1)}, u32[]{:S(2)}) copy-start(bf16[2048,128]{1,0:T(8,128)(2,1)} %x_ref.1) | copy-start | bytes 1572868
  1.7 1.0 %copy-start.1 = (bf16[2048,128]{1,0:T(8,128)(2,1)S(1)}, bf16[2048,128]{1,0:T(8,128)(2,1)}, u32[]{:S(2)}) copy-start(bf16[2048,128]{1,0:T(8,128)(2,1)} %gate_hbm.1) | copy-start | bytes 1572868
  2.7 1.0 %copy-start.2 = (bf16[2048,128]{1,0:T(8,128)(2,1)S(1)}, bf16[2048,128]{1,0:T(8,128)(2,1)}, u32[]{:S(2)}) copy-start(bf16[2048,128]{1,0:T(8,128)(2,1)} %up_hbm.1) | copy-start | bytes 1572868
  3.8 0.8 %copy-start.3 = (f32[64,64]{1,0:T(8,128)S(1)}, f32[64,64]{1,0:T(8,128)}, u32[]{:S(2)}) copy-start(f32[64,64]{1,0:T(8,128)} %raw_ref.1) | copy-start | bytes 49156
where the time goes:
time: 62.3 us; the launch traced here: 62 us
  Pallas kernels  55.2 us (89%)
  local copies, waits for them, and re-layouts  6.08 us (10%)
  between operations  0.65 us (1%)
    pallas_call x1, Pallas kernels, layered_shards(): pl.pallas_call(functools.partial(layered_kernel, seq_count, chan_count),...  55.2 us
    unnamed x11, local copies, waits for them, and re-layouts  6.08 us

commit v1 on v0

v1 whole, which is shorter than its diff:
```python
import functools
import math

import jax
import jax.numpy as jnp
from jax import lax
from jax.experimental import pallas as pl
from jax.experimental.pallas import tpu as pltpu
from jax.sharding import PartitionSpec as P

D = 4096
G = 64


HIGHEST = lax.Precision.HIGHEST


def make_tables(seq_count, block_len):
    outer = 2 * seq_count
    total = outer * block_len
    outer_index = jnp.arange(outer, dtype=jnp.int32)
    block_index = jnp.arange(seq_count, dtype=jnp.int32)
    inner_index = jnp.arange(block_len, dtype=jnp.int32)
    block_angle = (outer_index[:, None] * block_index[None, :] % outer).astype(jnp.float32) * (
        2.0 * math.pi / outer
    )
    twist_angle = (outer_index[:, None] * inner_index[None, :] % total).astype(jnp.float32) * (
        2.0 * math.pi / total
    )
    inner_angle = (inner_index[:, None] * inner_index[None, :] % block_len).astype(jnp.float32) * (
        2.0 * math.pi / block_len
    )
    return (
        jnp.cos(block_angle),
        jnp.sin(block_angle),
        jnp.cos(twist_angle),
        jnp.sin(twist_angle),
        jnp.cos(inner_angle),
        jnp.sin(inner_angle),
    )


def right_product(values, table):
    return jnp.einsum("ckm,mj->ckj", values, table, precision=HIGHEST)


def forward_dft(signal, tables):
    block_cos, block_sin, twist_cos, twist_sin, inner_cos, inner_sin = tables
    real_first = jnp.einsum("kn,cnm->ckm", block_cos, signal, precision=HIGHEST)
    imag_first = -jnp.einsum("kn,cnm->ckm", block_sin, signal, precision=HIGHEST)
    real_twist = real_first * twist_cos + imag_first * twist_sin
    imag_twist = imag_first * twist_cos - real_first * twist_sin
    real_spec = right_product(real_twist, inner_cos) + right_product(imag_twist, inner_sin)
    imag_spec = right_product(imag_twist, inner_cos) - right_product(real_twist, inner_sin)
    return (real_spec, imag_spec)


def inverse_dft(real_spec, imag_spec, tables):
    block_cos, block_sin, twist_cos, twist_sin, inner_cos, inner_sin = tables
    real_first = right_product(real_spec, inner_cos) - right_product(imag_spec, inner_sin)
    imag_first = right_product(real_spec, inner_sin) + right_product(imag_spec, inner_cos)
    real_twist = real_first * twist_cos - imag_first * twist_sin
    imag_twist = real_first * twist_sin + imag_first * twist_cos
    total = real_spec.shape[1] * real_spec.shape[2]
    result = jnp.einsum("kn,ckm->cnm", block_cos, real_twist, precision=HIGHEST)
    result = result - jnp.einsum("kn,ckm->cnm", block_sin, imag_twist, precision=HIGHEST)
    return result / total


def shards(inputs, gating, grad_out, filters):
    seq_count = lax.axis_size("seq")
    chan_count = lax.axis_size("chan")
    chan_rows, block_len = inputs.shape
    local_chan = chan_rows // seq_count
    group_width = D // G
    groups_here = G // chan_count
    local_groups = max(1, local_chan // group_width)
    group_share = local_chan // local_groups
    copies = max(1, seq_count // groups_here)
    length = block_len * seq_count
    outer = 2 * seq_count
    factor = 1.0 / math.sqrt(group_width * length)
    tables = make_tables(seq_count, block_len)
    whole = lax.all_gather(filters, ("seq", "chan"), axis=1, tiled=True)
    first_group = (
        lax.axis_index("chan") * chan_rows + lax.axis_index("seq") * local_chan
    ) // group_width
    kernel_rows = lax.dynamic_slice_in_dim(whole, first_group, local_groups, 0)
    kernel_blocks = kernel_rows.reshape(local_groups, seq_count, block_len)
    kernel_real, kernel_imag = forward_dft(kernel_blocks * factor, tables)
    kernel_real = kernel_real[:, None]
    kernel_imag = kernel_imag[:, None]
    shaped_inputs = inputs.reshape(chan_rows, 1, block_len)
    values, gate_part, upstream = (
        lax.all_to_all(shaped_inputs, "seq", split_axis=0, concat_axis=1, tiled=True),
        lax.all_to_all(
            gating.reshape(chan_rows, 1, block_len), "seq", split_axis=0, concat_axis=1, tiled=True
        ),
        lax.all_to_all(
            grad_out.reshape(chan_rows, 1, block_len),
            "seq",
            split_axis=0,
            concat_axis=1,
            tiled=True,
        ),
    )
    input_real, input_imag = forward_dft(values.astype(jnp.float32), tables)
    upstream_f = upstream.astype(jnp.float32)
    product_b = lax.optimization_barrier(
        (gate_part.astype(jnp.float32) * upstream_f).astype(jnp.bfloat16)
    )
    up_real, up_imag = forward_dft(product_b.astype(jnp.float32), tables)
    grouped_shape = (local_groups, group_share, outer, block_len)
    input_real = input_real.reshape(grouped_shape)
    input_imag = input_imag.reshape(grouped_shape)
    up_real = up_real.reshape(grouped_shape)
    up_imag = up_imag.reshape(grouped_shape)
    flat_shape = (local_chan, outer, block_len)
    conv_real = input_real * kernel_real - input_imag * kernel_imag
    conv_imag = input_real * kernel_imag + input_imag * kernel_real
    convolved = inverse_dft(conv_real.reshape(flat_shape), conv_imag.reshape(flat_shape), tables)
    conv_b = convolved.astype(jnp.bfloat16)
    second = (upstream_f * lax.optimization_barrier(conv_b).astype(jnp.float32)).astype(
        jnp.bfloat16
    )
    back_real = up_real * kernel_real + up_imag * kernel_imag
    back_imag = up_imag * kernel_real - up_real * kernel_imag
    grad_input = inverse_dft(
        back_real.reshape(flat_shape), back_imag.reshape(flat_shape), tables
    ).astype(jnp.bfloat16)
    returned_input, returned_second = (
        lax.all_to_all(grad_input, "seq", split_axis=1, concat_axis=0, tiled=True),
        lax.all_to_all(second, "seq", split_axis=1, concat_axis=0, tiled=True),
    )
    returned_second = returned_second.reshape(chan_rows, block_len)
    cross_real = jnp.sum(input_real * up_real + input_imag * up_imag, axis=1)
    cross_imag = jnp.sum(input_real * up_imag - input_imag * up_real, axis=1)
    partial_grad = inverse_dft(cross_real, cross_imag, tables) * factor
    received = lax.all_to_all(partial_grad, "seq", split_axis=1, concat_axis=0, tiled=True)
    summed = received.reshape(groups_here, copies, block_len).sum(axis=1)
    grad_filters = lax.all_to_all(summed, "chan", split_axis=1, concat_axis=0, tiled=True)
    return (returned_input.reshape(chan_rows, block_len), returned_second, grad_filters)


GROUP_WIDTH = D // G
MESH = pl.DeviceIdType.MESH
TILE = 256
LAYERS = 4
DELAY_COMPUTE, DELAY_FINISH = 2, 4
SPLIT_LAG = 4
NT = (((1,), (1,)), ((), ()))
NN = (((1,), (0,)), ((), ()))


def dot(a, b, dims):
    return lax.dot_general(a, b, dims, preferred_element_type=jnp.float32)


def layered_kernel(
    seq_count,
    chan_count,
    x_hbm,
    gate_hbm,
    up_hbm,
    raw_hbm,
    gi_ref,
    gg_ref,
    grad_ref,
    gate_ref,
    up_ref,
    raw_ref,
    filt_ref,
    filt_in,
    filt_all,
    u_loc,
    xs,
    us,
    table,
    acc_c,
    acc_g,
    cv,
    gv,
    conv_in,
    held,
    part_out,
    part_in,
    fg_out,
    fg_layer,
    fg_sum,
    fg_in,
    load_sem,
    x_send,
    u_send,
    c_send,
    g_send,
    z_send,
    p_send,
    f_send,
    k_send,
    x_recv,
    u_recv,
    c_recv,
    g_recv,
    z_recv,
    p_recv,
    f_recv,
    fz_recv,
    k_recv,
    kz_recv,
):
    seq = lax.axis_index("seq")
    chan = lax.axis_index("chan")
    peers = seq_count // LAYERS
    crew = peers * chan_count
    layer = seq // peers
    spot = lax.rem(seq, peers)
    slot = spot * chan_count + chan
    last = LAYERS - 1
    groups = xs.shape[0]
    block = x_hbm.shape[1]
    per_tile = TILE // block
    length = block * seq_count
    tiles = length // TILE
    half = tiles // LAYERS
    width = GROUP_WIDTH
    layer_rows = half * width
    local_chan = groups * width
    share = raw_hbm.shape[1]
    factor = 1.0 / math.sqrt(width * length)

    loads = [
        pltpu.make_async_copy(gate_hbm, gate_ref, load_sem.at[0]),
        pltpu.make_async_copy(up_hbm, up_ref, load_sem.at[1]),
        pltpu.make_async_copy(raw_hbm, raw_ref, load_sem.at[2]),
    ]
    for load in loads:
        load.start()

    barrier = pltpu.get_barrier_semaphore()

    def greet(to_seq, to_chan):
        pl.semaphore_signal(barrier, inc=1, device_id=(to_seq, to_chan), device_id_type=MESH)

    def crew_member(k):
        other = lax.rem(slot + k, crew)
        return other // chan_count, lax.rem(other, chan_count)

    for k in range(1, LAYERS):
        greet(lax.rem(layer + k, LAYERS) * peers + spot, chan)
    for k in range(1, crew):
        p, c = crew_member(k)
        greet(layer * peers + p, c)

    us[:, tiles * width :, :] = jnp.zeros((groups, us.shape[1] - tiles * width, TILE), jnp.bfloat16)
    for which in (0, 1):
        span = slice((1 - which) * layer_rows, (2 - which) * layer_rows)

        @pl.when(layer == which)
        def _(span=span):
            us[:, span, :] = jnp.zeros((groups, layer_rows, TILE), jnp.bfloat16)

    loads[2].wait()
    scaled = raw_ref[...] * factor
    lanes = jnp.concatenate([scaled] * chan_count, axis=1)
    kept = lax.broadcasted_iota(jnp.int32, lanes.shape, 1) // share == chan
    lanes = jnp.where(kept, lanes, 0.0)
    for i in range(crew):
        filt_ref[i] = lanes[i * groups : (i + 1) * groups, :]
    loads[0].wait()
    loads[1].wait()
    u_loc[...] = (
        gate_ref[...].astype(jnp.float32) * up_ref[...].astype(jnp.float32)
    ).astype(jnp.bfloat16)
    pl.semaphore_wait(barrier, crew + LAYERS - 2)

    def place(ref, g, s):
        return ref.at[
            g,
            pl.ds(pl.multiple_of((s // per_tile) * width, width), width),
            pl.ds(pl.multiple_of(lax.rem(s, per_tile) * block, block), block),
        ]

    def strip(ref, q, g):
        return ref.at[pl.ds(pl.multiple_of(q * local_chan + g * width, width), width), :]

    def remote(from_ref, to_ref, send, recv, to_seq, to_chan=None):
        return pltpu.make_async_remote_copy(
            src_ref=from_ref,
            dst_ref=to_ref,
            send_sem=send,
            recv_sem=recv,
            device_id=(to_seq, chan if to_chan is None else to_chan),
            device_id_type=MESH,
        )

    def wait_bytes(ref, sem):
        pltpu.make_async_copy(ref, ref, sem).wait()

    def layer_span(ref, g, which):
        return ref.at[g, pl.ds(pl.multiple_of(which * layer_rows, layer_rows), layer_rows), :]

    def scatter(ref, buf, send, recv, g):
        for k in (2, 3, 1):
            p = lax.rem(spot + k, peers)
            remote(
                strip(ref, p, g), place(buf, g, seq), send.at[0], recv.at[g], layer * peers + p
            ).start()
        pltpu.make_async_copy(strip(ref, spot, g), place(buf, g, seq), recv.at[g]).start()

    def scatter_both(g):
        @pl.when(layer < LAYERS // 2)
        def _():
            scatter(x_hbm, xs, x_send, x_recv, g)
            scatter(u_loc, us, u_send, u_recv, g)

        @pl.when(layer >= LAYERS // 2)
        def _():
            scatter(u_loc, us, u_send, u_recv, g)
            scatter(x_hbm, xs, x_send, x_recv, g)

    def give_back(buf, ref, send, recv, g):
        for k in (2, 3, 1):
            p = lax.rem(spot + k, peers)
            remote(
                place(buf, g, p), strip(ref, spot, g), send.at[0], recv.at[0], layer * peers + p
            ).start()
        pltpu.make_async_copy(place(buf, g, spot), strip(ref, spot, g), recv.at[0]).start()

    def hop(g, origin, to_layer):
        buf = xs if origin < LAYERS // 2 else us
        ref = layer_span(buf, g, origin)
        return remote(ref, ref, z_send.at[0], z_recv.at[g, origin], to_layer * peers + spot)

    def hand(g, to_layer):
        return remote(
            part_out.at[g], part_in.at[g], p_send.at[0], p_recv.at[g], to_layer * peers + spot
        )

    scatter_both(0)
    for k in range(1, crew):
        p, c = crew_member(k)
        remote(
            filt_ref.at[c * peers + p], filt_in.at[slot], k_send.at[0], k_recv.at[0],
            layer * peers + p, c,
        ).start()
    pltpu.make_async_copy(filt_ref.at[chan * peers + spot], filt_in.at[slot], k_recv.at[0]).start()

    def scatter_rest(g, carry):
        scatter_both(g)
        return carry

    lax.fori_loop(1, groups, scatter_rest, 0)

    filt_targets = {0: (1, 2, 3), 1: (2,), 2: (1,), 3: (1, 2)}
    filt_sources = {0: (), 1: (0, 2, 3), 2: (0, 1, 3), 3: (0,)}

    def filt_hop(origin, to_layer):
        return remote(
            filt_all.at[origin], filt_all.at[origin], f_send.at[1], kz_recv.at[origin],
            to_layer * peers + spot,
        )

    def spread_filters():
        wait_bytes(filt_in, k_recv.at[0])
        for s in range(peers):
            part = filt_in[s * chan_count]
            for c in range(1, chan_count):
                part = part + filt_in[s * chan_count + c]
            filt_all[layer, s] = part
        for which in range(LAYERS):

            @pl.when(layer == which)
            def _(which=which):
                for to in filt_targets[which]:
                    filt_hop(which, to).start()

    def gather_layer(g):
        first_x = layer < LAYERS // 2

        @pl.when(first_x)
        def _():
            wait_bytes(layer_span(xs, g, layer), x_recv.at[g])

        @pl.when(jnp.logical_not(first_x))
        def _():
            wait_bytes(layer_span(us, g, layer), u_recv.at[g])

        @pl.when(layer == 0)
        def _():
            hop(g, 0, 2).start()
            hop(g, 0, 1).start()

        @pl.when(layer == 1)
        def _():
            hop(g, 1, 2).start()

        @pl.when(layer == 2)
        def _():
            hop(g, 2, 1).start()

        @pl.when(layer == 3)
        def _():
            hop(g, 3, 1).start()
            hop(g, 3, 2).start()

        @pl.when(g == 0)
        def _():
            spread_filters()

    row_id = lax.broadcasted_iota(jnp.int32, (TILE, TILE), 0)
    col_id = lax.broadcasted_iota(jnp.int32, (TILE, TILE), 1)
    flip = jnp.where(row_id + col_id == TILE - 1, 1.0, 0.0).astype(jnp.bfloat16)
    row_in = lax.broadcasted_iota(jnp.int32, (block, block), 0)
    col_in = lax.broadcasted_iota(jnp.int32, (block, block), 1)
    upper = col_in >= row_in
    lower_flipped = col_in + row_in >= block - 1

    def compute(g):
        for which in range(LAYERS):

            @pl.when(layer == which)
            def _(which=which):
                compute_for(which, g)

    def compute_for(which, g):
        low_end, high_end = which * half, (which + 1) * half - 1
        inner = which in (1, 2)
        x_first = 0 if which in (1, 2) else low_end
        u_last = tiles - 1 if which in (1, 2) else high_end
        conv_last = tiles - 1 if which == 2 else high_end
        grad_first = 0 if which == 1 else low_end

        @pl.when(g == 0)
        def _():
            for origin in filt_sources[which]:
                filt_hop(origin, which).wait_recv()

        if which < LAYERS // 2:
            wait_bytes(layer_span(us, g, which), u_recv.at[g])
        else:
            wait_bytes(layer_span(xs, g, which), x_recv.at[g])
        if inner:
            for origin in range(LAYERS):
                if origin != which:
                    hop(g, origin, which).wait_recv()

        def span(first, final):
            return slice(first * width, (final + 1) * width)

        lags = [
            lag
            for lag in range(tiles)
            if max(x_first, low_end - lag) <= min(high_end, conv_last - lag)
            or max(low_end, grad_first + lag) <= min(u_last, high_end + lag)
        ]
        before = jnp.zeros((block, block), jnp.float32)
        for m in range(per_tile * len(lags)):
            row = filt_all[m // peers, m % peers, pl.ds(g, 1), :]
            rolled = pltpu.roll(
                jnp.broadcast_to(row, (block, block)), 0, 1, stride=1, stride_axis=0
            )
            table[m] = jnp.where(upper, rolled, before).astype(jnp.bfloat16)
            before = rolled

        def gather_table(lag):
            rows = []
            for i in range(per_tile):
                parts = []
                for j in range(per_tile):
                    m = lag * per_tile + j - i
                    parts.append(table[m] if m >= 0 else jnp.zeros((block, block), jnp.bfloat16))
                rows.append(jnp.concatenate(parts, axis=1))
            return jnp.concatenate(rows, axis=0)

        def add(acc, seen, first, final, value):
            runs = []
            for tile in range(first, final + 1):
                if runs and runs[-1][2] == (tile in seen):
                    runs[-1][1] = tile
                else:
                    runs.append([tile, tile, tile in seen])
            for begin, end, known in runs:
                part = value[(begin - first) * width : (end - first + 1) * width]
                if known:
                    acc[span(begin, end), :] += part
                else:
                    acc[span(begin, end), :] = part
            seen.update(range(first, final + 1))

        seen_c, seen_g = set(), set()
        for lag in lags:
            filt = gather_table(lag)
            first, final = max(x_first, low_end - lag), min(high_end, conv_last - lag)
            u_from, u_to = max(low_end, grad_first + lag), min(u_last, high_end + lag)
            if first <= final:
                add(acc_c, seen_c, first + lag, final + lag, dot(xs[g, span(first, final), :], filt, NN))
            if u_from <= u_to:
                add(acc_g, seen_g, u_from - lag, u_to - lag, dot(us[g, span(u_from, u_to), :], filt, NT))

        mine = span(low_end, high_end)
        if which == 2:
            part_out[g] = acc_c[last * layer_rows :, :].astype(jnp.bfloat16)
            hand(g, 3).start()
        if which == 1:
            part_out[g] = acc_g[:layer_rows, :].astype(jnp.bfloat16)
            hand(g, 0).start()
        if which < last:
            cv[g] = acc_c[mine, :].astype(jnp.bfloat16)
            give_back(cv, conv_in, c_send, c_recv, g)
        else:
            held[g] = acc_c[mine, :]
        if which > 0:
            gv[g] = acc_g[mine, :].astype(jnp.bfloat16)
            give_back(gv, gi_ref, g_send, g_recv, g)
        else:
            held[g] = acc_g[mine, :]

        gram_first = 0 if inner else low_end
        turned = dot(flip, xs[g, span(gram_first, high_end), :], NT).astype(jnp.bfloat16)

        def window(first, count):
            return us[g, first * width : (first + count) * width, :]

        def gram_of(lag):
            if not inner:
                return dot(turned, window(low_end + lag, half), NN)
            if which == 1:
                return dot(turned, window(lag, 2 * half), NN)
            if lag < SPLIT_LAG:
                return dot(turned[:, 2 * half * width :], window(2 * half + lag, half), NN)
            return dot(turned[:, : 2 * half * width], window(lag, 2 * half), NN)

        gram_lags = half if not inner else (SPLIT_LAG if which == 1 else tiles)
        zero = jnp.zeros((block, block), jnp.float32)
        gram = gram_of(0)
        current = gram[block:, :block] + gram[:block, block:]
        for lag in range(gram_lags):
            following = gram_of(lag + 1) if lag + 1 < gram_lags else None
            odd = gram[block:, block:]
            if following is None:
                even = zero
            else:
                odd = odd + following[:block, :block]
                even = following[block:, :block] + following[:block, block:]
            for i, (a, b) in enumerate(((current, odd), (odd, even))):
                mixed = jnp.where(lower_flipped, a, b)
                aligned = pltpu.roll(mixed, 1, 1, stride=1, stride_axis=0)
                total = jnp.sum(aligned, axis=0, keepdims=True) * factor
                fg_out[lag * per_tile + i, pl.ds(g, 1), :] = total
            current, gram = even, following

        @pl.when(g == groups - 1)
        def _():
            for to in grad_targets[which]:
                grad_hop(which, to).start()

    grad_targets = {0: (), 1: (0,), 2: (0, 1, 3), 3: (0,)}
    grad_sources = {0: (1, 2, 3), 1: (2,), 2: (), 3: (2,)}

    def grad_hop(origin, to_layer):
        return remote(
            fg_out.at[pl.ds(to_layer * peers, peers)], fg_layer.at[origin], f_send.at[0],
            fz_recv.at[origin], to_layer * peers + spot,
        )

    def finish(g):
        @pl.when(layer == last)
        def _():
            hand(g, last).wait_recv()
            cv[g] = (held[g] + part_in[g].astype(jnp.float32)).astype(jnp.bfloat16)
            give_back(cv, conv_in, c_send, c_recv, g)

        @pl.when(layer == 0)
        def _():
            hand(g, 0).wait_recv()
            gv[g] = (held[g] + part_in[g].astype(jnp.float32)).astype(jnp.bfloat16)
            give_back(gv, gi_ref, g_send, g_recv, g)

    def stage(step, delay, body):
        @pl.when((step >= delay) & (step < groups + delay))
        def _():
            body(step - delay)

    def pipeline(step, carry):
        stage(step, 0, gather_layer)
        stage(step, DELAY_COMPUTE, compute)
        stage(step, DELAY_FINISH, finish)
        return carry

    lax.fori_loop(0, groups + DELAY_FINISH, pipeline, 0)

    for which in range(LAYERS):

        @pl.when(layer == which)
        def _(which=which):
            total = None
            if which != 3:
                total = fg_out[which * peers : (which + 1) * peers]
            for origin in grad_sources[which]:
                grad_hop(origin, which).wait_recv()
                part = fg_layer[origin]
                total = part if total is None else total + part
            fg_sum[...] = total

    for k in range(1, crew):
        p, c = crew_member(k)
        remote(
            fg_sum.at[p], fg_in.at[chan * peers + spot], f_send.at[2], f_recv.at[0],
            layer * peers + p, c,
        ).start()
    pltpu.make_async_copy(fg_sum.at[spot], fg_in.at[chan * peers + spot], f_recv.at[0]).start()

    wait_bytes(conv_in, c_recv.at[0])
    gg_ref[...] = (up_ref[...].astype(jnp.float32) * conv_in[...].astype(jnp.float32)).astype(
        jnp.bfloat16
    )
    wait_bytes(gi_ref, g_recv.at[0])
    wait_bytes(fg_in, f_recv.at[0])
    for i in range(crew):
        total = fg_in[i]
        kept_part = total[:, :share]
        for d in range(1, chan_count):
            kept_part = jnp.where(chan == d, total[:, d * share : (d + 1) * share], kept_part)
        grad_ref[i * groups : (i + 1) * groups, :] = kept_part

    sent = pl.ds(0, groups * (peers - 1) // peers)
    wait_bytes(cv.at[sent], x_send.at[0])
    wait_bytes(cv.at[sent], u_send.at[0])
    wait_bytes(cv.at[sent], c_send.at[0])
    wait_bytes(cv.at[sent], g_send.at[0])
    wait_bytes(filt_in.at[pl.ds(0, crew - 1)], k_send.at[0])
    wait_bytes(filt_in.at[pl.ds(0, crew - 1)], f_send.at[2])
    for which in range(LAYERS):

        @pl.when(layer == which)
        def _(which=which):
            hops = 1 if which in (1, 2) else 2
            for _ in range(hops):
                wait_bytes(cv, z_send.at[0])
            if which in (1, 2):
                wait_bytes(cv, p_send.at[0])
            for _ in filt_targets[which]:
                wait_bytes(filt_all.at[0], f_send.at[1])
            for _ in grad_targets[which]:
                wait_bytes(fg_layer.at[0], f_send.at[0])


def store_kernel(a_ref, b_ref, c_ref, a_out, b_out, c_out, sems):
    copies = [
        pltpu.make_async_copy(a_ref, a_out, sems.at[0]),
        pltpu.make_async_copy(b_ref, b_out, sems.at[1]),
        pltpu.make_async_copy(c_ref, c_out, sems.at[2]),
    ]
    for copy in copies:
        copy.start()
    for copy in copies:
        copy.wait()


def layered_shards(inputs, gating, grad_out, filters):
    seq_count = lax.axis_size("seq")
    chan_count = lax.axis_size("chan")
    chan_rows, block = inputs.shape
    peers = seq_count // LAYERS
    crew = peers * chan_count
    groups = chan_rows // peers // GROUP_WIDTH
    length = block * seq_count
    tiles = length // TILE
    rows = tiles * GROUP_WIDTH
    layer_rows = rows // LAYERS
    blocks = length // block
    vmem = pl.BlockSpec(memory_space=pltpu.VMEM)
    hbm = pl.BlockSpec(memory_space=pltpu.HBM)
    single = pltpu.SemaphoreType.DMA((1,))
    by_group = pltpu.SemaphoreType.DMA((groups,))
    by_layer = pltpu.SemaphoreType.DMA((LAYERS,))
    flat = pltpu.VMEM((chan_rows, block), jnp.bfloat16)
    layered = pltpu.VMEM((groups, layer_rows, TILE), jnp.bfloat16)
    small = pltpu.VMEM((crew, groups, block), jnp.float32)
    outs = (
        jax.ShapeDtypeStruct((chan_rows, block), jnp.bfloat16),
        jax.ShapeDtypeStruct((chan_rows, block), jnp.bfloat16),
        jax.ShapeDtypeStruct(filters.shape, jnp.float32),
    )
    results = pl.pallas_call(
        functools.partial(layered_kernel, seq_count, chan_count),
        out_shape=outs,
        in_specs=[hbm] * 4,
        out_specs=(vmem, vmem, vmem),
        scratch_shapes=[
            flat,
            flat,
            pltpu.VMEM(filters.shape, jnp.float32),
            small,
            small,
            pltpu.VMEM((LAYERS, peers, groups, block), jnp.float32),
            flat,
            pltpu.VMEM((groups, rows, TILE), jnp.bfloat16),
            pltpu.VMEM((groups, rows + 2 * layer_rows, TILE), jnp.bfloat16),
            pltpu.VMEM((blocks, block, block), jnp.bfloat16),
            pltpu.VMEM((rows, TILE), jnp.float32),
            pltpu.VMEM((rows, TILE), jnp.float32),
            layered,
            layered,
            flat,
            pltpu.VMEM((groups, layer_rows, TILE), jnp.float32),
            layered,
            layered,
            pltpu.VMEM((blocks, groups, block), jnp.float32),
            pltpu.VMEM((LAYERS, peers, groups, block), jnp.float32),
            pltpu.VMEM((peers, groups, block), jnp.float32),
            small,
            pltpu.SemaphoreType.DMA((3,)),
            single,
            single,
            single,
            single,
            single,
            single,
            pltpu.SemaphoreType.DMA((3,)),
            single,
            by_group,
            by_group,
            single,
            single,
            pltpu.SemaphoreType.DMA((groups, LAYERS)),
            by_group,
            single,
            by_layer,
            single,
            by_layer,
        ],
        compiler_params=pltpu.CompilerParams(
            collective_id=0, has_side_effects=True, vmem_limit_bytes=VMEM_LIMIT
        ),
    )(inputs, gating, grad_out, filters)
    return pl.pallas_call(
        store_kernel,
        out_shape=outs,
        in_specs=[vmem] * 3,
        out_specs=(hbm, hbm, hbm),
        scratch_shapes=[pltpu.SemaphoreType.DMA((3,))],
    )(*results)


VMEM_LIMIT = 56 * 1024 * 1024


def solution(mesh):
    placed = (P("chan", "seq"), P("chan", "seq"), P("chan", "seq"), P(None, ("seq", "chan")))
    layered = mesh.shape["seq"] == 16 and mesh.shape["chan"] == 2
    return jax.shard_map(
        layered_shards if layered else shards,
        mesh=mesh,
        in_specs=placed,
        out_specs=(P("chan", "seq"), P("chan", "seq"), P(None, ("seq", "chan"))),
        check_vma=False,
    )
```

time: 62.3 us -> 47.6 us (0.76)
  Pallas kernels: 55.2 us -> 46.8 us
  local copies, waits for them, and re-layouts: 6.08 us -> 0 us
    pallas_call x1, Pallas kernels: 55.2 us -> 44.6 us  [layered_shards(): pl.pallas_call(functools.partial(layered_kernel, seq_count, chan_count),...]
    unnamed x11 -> x0, local copies, waits for them, and re-layouts: 6.08 us -> none
    pallas_call x0 -> x1, Pallas kernels: none -> 2.2 us  [layered_shards(): pl.pallas_call(store_kernel, out_shape=outs, in_specs=[vmem] * 3, out_spe...]
where the time goes in v1:
time: 47.6 us; the launch traced here: 47.5 us
  Pallas kernels  46.8 us (98%)
  between operations  0.64 us (1%)
    pallas_call x1, Pallas kernels, layered_shards(): pl.pallas_call(functools.partial(layered_kernel, seq_count, chan_count),...  44.6 us
    pallas_call x1, Pallas kernels, layered_shards(): pl.pallas_call(store_kernel, out_shape=outs, in_specs=[vmem] * 3, out_spe...  2.2 us

profile of v1, /device:TPU:0, one launch (start us, length us, event | category | flops | bytes accessed | tf_op | source)
XLA Modules:
  0.0 47.5 jit_solution(12288436547955745369)
XLA Ops:
  0.6 44.6 %shard_map.67 = (bf16[2048,128]{1,0:T(8,128)(2,1)}, bf16[2048,128]{1,0:T(8,128)(2,1)}, f32[64,64]{1,0:T(8,128)}) custom-call(bf16[2048,128]{1,0:T(8,128)(2,1)} %x_hbm.1, bf16[2048,128]{1,0:T(8,128)(2,1)} %gate_hbm.1, bf16[2048,128]{1,0:T(8,128)(2,1)} %up_hbm.1, f32[64,64]{1,0:T(8,128)} %raw_hbm.1), custom_call_target="tpu_custom_call" | custom-call | tf_op jit(solution)/shard_map/pallas_call | solution.py:685
  45.3 2.2 %shard_map.68 = (bf16[2048,128]{1,0:T(8,128)(2,1)}, bf16[2048,128]{1,0:T(8,128)(2,1)}, f32[64,64]{1,0:T(8,128)}) custom-call(bf16[2048,128]{1,0:T(8,128)(2,1)} %get-tuple-element.6.a_ref, bf16[2048,128]{1,0:T(8,128)(2,1)} %get-tuple-element.7.b_ref, f32[64,64]{1,0:T(8,128)} %get-tuple-element.8.c_ref), custom_call_target="tpu_custom_call" | custom-call | tf_op jit(solution)/shard_map/pallas_call | solution.py:737

commit v2 on v1

--- a/solution.py
+++ b/solution.py
@@ -146,8 +146,7 @@
 MESH = pl.DeviceIdType.MESH
 TILE = 256
 LAYERS = 4
-DELAY_COMPUTE, DELAY_FINISH = 2, 4
-SPLIT_LAG = 4
+LEAD, DELAY_RELAY, DELAY_COMPUTE = 4, 2, 3
 NT = (((1,), (1,)), ((), ()))
 NN = (((1,), (0,)), ((), ()))
 
@@ -171,6 +170,7 @@
     raw_ref,
     filt_ref,
     filt_in,
+    filt_layer,
     filt_all,
     u_loc,
     xs,
@@ -181,9 +181,7 @@
     cv,
     gv,
     conv_in,
-    held,
-    part_out,
-    part_in,
+    far,
     fg_out,
     fg_layer,
     fg_sum,
@@ -194,19 +192,20 @@
     c_send,
     g_send,
     z_send,
-    p_send,
+    far_send,
     f_send,
     k_send,
     x_recv,
     u_recv,
     c_recv,
     g_recv,
-    z_recv,
-    p_recv,
+    zx_recv,
+    zu_recv,
     f_recv,
     fz_recv,
     k_recv,
     kz_recv,
+    enter_sem,
 ):
     seq = lax.axis_index("seq")
     chan = lax.axis_index("chan")
@@ -245,19 +244,23 @@
         other = lax.rem(slot + k, crew)
         return other // chan_count, lax.rem(other, chan_count)
 
-    for k in range(1, LAYERS):
-        greet(lax.rem(layer + k, LAYERS) * peers + spot, chan)
     for k in range(1, crew):
         p, c = crew_member(k)
         greet(layer * peers + p, c)
-
-    us[:, tiles * width :, :] = jnp.zeros((groups, us.shape[1] - tiles * width, TILE), jnp.bfloat16)
-    for which in (0, 1):
-        span = slice((1 - which) * layer_rows, (2 - which) * layer_rows)
+    everyone, lone = range(peers), (spot,)
+    greeted = {
+        0: ((1, everyone), (2, lone)),
+        1: ((0, lone), (2, lone), (3, lone)),
+        2: ((0, lone), (1, lone), (3, everyone)),
+        3: (),
+    }
+    for which in range(LAYERS):
 
         @pl.when(layer == which)
-        def _(span=span):
-            us[:, span, :] = jnp.zeros((groups, layer_rows, TILE), jnp.bfloat16)
+        def _(which=which):
+            for to_layer, spots in greeted[which]:
+                for p in spots:
+                    greet(to_layer * peers + p, chan)
 
     loads[2].wait()
     scaled = raw_ref[...] * factor
@@ -271,7 +274,25 @@
     u_loc[...] = (
         gate_ref[...].astype(jnp.float32) * up_ref[...].astype(jnp.float32)
     ).astype(jnp.bfloat16)
-    pl.semaphore_wait(barrier, crew + LAYERS - 2)
+    expected = {0: 2, 1: peers + 1, 2: 2, 3: 1 + peers}
+    for which in range(LAYERS):
+
+        @pl.when(layer == which)
+        def _(which=which):
+            pl.semaphore_wait(barrier, crew - 1 + expected[which])
+
+    def enter(origin, to_layer, p):
+        pl.semaphore_signal(
+            enter_sem.at[origin],
+            inc=1,
+            device_id=(to_layer * peers + p, chan),
+            device_id_type=MESH,
+        )
+
+    @pl.when(layer == 3)
+    def _():
+        for p in everyone:
+            enter(3, 2, p)
 
     def place(ref, g, s):
         return ref.at[
@@ -326,17 +347,62 @@
             ).start()
         pltpu.make_async_copy(place(buf, g, spot), strip(ref, spot, g), recv.at[0]).start()
 
-    def hop(g, origin, to_layer):
-        buf = xs if origin < LAYERS // 2 else us
-        ref = layer_span(buf, g, origin)
-        return remote(ref, ref, z_send.at[0], z_recv.at[g, origin], to_layer * peers + spot)
-
-    def hand(g, to_layer):
-        return remote(
-            part_out.at[g], part_in.at[g], p_send.at[0], p_recv.at[g], to_layer * peers + spot
+    def send_far(g, ref, recv, to_layer):
+        for k in (2, 3, 1, 0):
+            p = lax.rem(spot + k, peers)
+            remote(
+                place(far, g, p), strip(ref, spot, g), far_send.at[0], recv.at[0],
+                to_layer * peers + p,
+            ).start()
+
+    def hop_x(g, origin, to_layer):
+        ref = layer_span(xs, g, origin)
+        return remote(ref, ref, z_send.at[0], zx_recv.at[g, origin], to_layer * peers + spot)
+
+    def hop_u(g, origin, to_layer):
+        ref = layer_span(us, g, origin)
+        return remote(ref, ref, z_send.at[0], zu_recv.at[g, origin], to_layer * peers + spot)
+
+    def ahead(from_ref, buf, recv, origin, to_layer):
+        def step(g, carry):
+            remote(
+                strip(from_ref, spot, g), place(buf, g, seq), z_send.at[0], recv.at[g, origin],
+                to_layer * peers + spot,
+            ).start()
+            return carry
+
+        lax.fori_loop(0, groups, step, 0)
+
+    def rest(g, buf, recv, origin, to_layer):
+        sibling = spot + 1 - 2 * lax.rem(spot, per_tile)
+        tile = origin * half + 1 - spot // per_tile
+        refs = (
+            place(buf, g, origin * peers + sibling),
+            buf.at[g, pl.ds(pl.multiple_of(tile * width, width), width), :],
         )
+        for ref in refs:
+            remote(
+                ref, ref, z_send.at[0], recv.at[g, origin], to_layer * peers + spot
+            ).start()
 
     scatter_both(0)
+
+    @pl.when(layer == 0)
+    def _():
+        ahead(x_hbm, xs, zx_recv, 0, 1)
+
+    @pl.when(layer == 1)
+    def _():
+        ahead(x_hbm, xs, zx_recv, 1, 2)
+
+    @pl.when(layer == 2)
+    def _():
+        ahead(u_loc, us, zu_recv, 2, 1)
+
+    @pl.when(layer == 3)
+    def _():
+        ahead(u_loc, us, zu_recv, 3, 2)
+
     for k in range(1, crew):
         p, c = crew_member(k)
         remote(
@@ -345,28 +411,32 @@
         ).start()
     pltpu.make_async_copy(filt_ref.at[chan * peers + spot], filt_in.at[slot], k_recv.at[0]).start()
 
-    def scatter_rest(g, carry):
+    def scatter_early(g, carry):
         scatter_both(g)
         return carry
 
-    lax.fori_loop(1, groups, scatter_rest, 0)
-
-    filt_targets = {0: (1, 2, 3), 1: (2,), 2: (1,), 3: (1, 2)}
+    lax.fori_loop(1, LEAD, scatter_early, 0)
+
+    filt_targets = {0: (1, 2), 1: (2,), 2: (1,), 3: (1, 2)}
     filt_sources = {0: (), 1: (0, 2, 3), 2: (0, 1, 3), 3: (0,)}
 
     def filt_hop(origin, to_layer):
         return remote(
-            filt_all.at[origin], filt_all.at[origin], f_send.at[1], kz_recv.at[origin],
+            filt_layer.at[origin], filt_layer.at[origin], f_send.at[1], kz_recv.at[origin],
             to_layer * peers + spot,
         )
 
     def spread_filters():
         wait_bytes(filt_in, k_recv.at[0])
+        parts = []
         for s in range(peers):
             part = filt_in[s * chan_count]
             for c in range(1, chan_count):
                 part = part + filt_in[s * chan_count + c]
-            filt_all[layer, s] = part
+            parts.append(part)
+        for s in range(peers // 2):
+            pair = jnp.concatenate(parts[2 * s : 2 * s + 2], axis=0)
+            filt_layer[layer, s] = pair.astype(jnp.bfloat16)
         for which in range(LAYERS):
 
             @pl.when(layer == which)
@@ -374,38 +444,51 @@
                 for to in filt_targets[which]:
                     filt_hop(which, to).start()
 
+    def wait_x(g):
+        wait_bytes(layer_span(xs, g, layer), x_recv.at[g])
+
+    def wait_u(g):
+        wait_bytes(layer_span(us, g, layer), u_recv.at[g])
+
     def gather_layer(g):
-        first_x = layer < LAYERS // 2
-
-        @pl.when(first_x)
-        def _():
-            wait_bytes(layer_span(xs, g, layer), x_recv.at[g])
-
-        @pl.when(jnp.logical_not(first_x))
-        def _():
-            wait_bytes(layer_span(us, g, layer), u_recv.at[g])
-
         @pl.when(layer == 0)
         def _():
-            hop(g, 0, 2).start()
-            hop(g, 0, 1).start()
+            wait_x(g)
+            rest(g, xs, zx_recv, 0, 1)
+            wait_u(g)
+            hop_u(g, 0, 1).start()
 
         @pl.when(layer == 1)
         def _():
-            hop(g, 1, 2).start()
+            wait_x(g)
+            rest(g, xs, zx_recv, 1, 2)
 
         @pl.when(layer == 2)
         def _():
-            hop(g, 2, 1).start()
+            wait_u(g)
+            rest(g, us, zu_recv, 2, 1)
 
         @pl.when(layer == 3)
         def _():
-            hop(g, 3, 1).start()
-            hop(g, 3, 2).start()
+            wait_u(g)
+            rest(g, us, zu_recv, 3, 2)
+            wait_x(g)
+            hop_x(g, 3, 2).start()
 
         @pl.when(g == 0)
         def _():
             spread_filters()
+
+    def relay(g):
+        @pl.when(layer == 1)
+        def _():
+            hop_x(g, 0, 1).wait_recv()
+            hop_x(g, 0, 2).start()
+
+        @pl.when(layer == 2)
+        def _():
+            hop_u(g, 3, 2).wait_recv()
+            hop_u(g, 3, 1).start()
 
     row_id = lax.broadcasted_iota(jnp.int32, (TILE, TILE), 0)
     col_id = lax.broadcasted_iota(jnp.int32, (TILE, TILE), 1)
@@ -422,39 +505,12 @@
             def _(which=which):
                 compute_for(which, g)
 
-    def compute_for(which, g):
-        low_end, high_end = which * half, (which + 1) * half - 1
-        inner = which in (1, 2)
-        x_first = 0 if which in (1, 2) else low_end
-        u_last = tiles - 1 if which in (1, 2) else high_end
-        conv_last = tiles - 1 if which == 2 else high_end
-        grad_first = 0 if which == 1 else low_end
-
-        @pl.when(g == 0)
-        def _():
-            for origin in filt_sources[which]:
-                filt_hop(origin, which).wait_recv()
-
-        if which < LAYERS // 2:
-            wait_bytes(layer_span(us, g, which), u_recv.at[g])
-        else:
-            wait_bytes(layer_span(xs, g, which), x_recv.at[g])
-        if inner:
-            for origin in range(LAYERS):
-                if origin != which:
-                    hop(g, origin, which).wait_recv()
-
-        def span(first, final):
-            return slice(first * width, (final + 1) * width)
-
-        lags = [
-            lag
-            for lag in range(tiles)
-            if max(x_first, low_end - lag) <= min(high_end, conv_last - lag)
-            or max(low_end, grad_first + lag) <= min(u_last, high_end + lag)
-        ]
+    def span(first, final):
+        return slice(first * width, (final + 1) * width)
+
+    def make_table(g, lags):
         before = jnp.zeros((block, block), jnp.float32)
-        for m in range(per_tile * len(lags)):
+        for m in range(per_tile * lags):
             row = filt_all[m // peers, m % peers, pl.ds(g, 1), :]
             rolled = pltpu.roll(
                 jnp.broadcast_to(row, (block, block)), 0, 1, stride=1, stride_axis=0
@@ -462,80 +518,75 @@
             table[m] = jnp.where(upper, rolled, before).astype(jnp.bfloat16)
             before = rolled
 
-        def gather_table(lag):
-            rows = []
-            for i in range(per_tile):
-                parts = []
-                for j in range(per_tile):
-                    m = lag * per_tile + j - i
-                    parts.append(table[m] if m >= 0 else jnp.zeros((block, block), jnp.bfloat16))
-                rows.append(jnp.concatenate(parts, axis=1))
-            return jnp.concatenate(rows, axis=0)
-
-        def add(acc, seen, first, final, value):
-            runs = []
-            for tile in range(first, final + 1):
-                if runs and runs[-1][2] == (tile in seen):
-                    runs[-1][1] = tile
-                else:
-                    runs.append([tile, tile, tile in seen])
-            for begin, end, known in runs:
-                part = value[(begin - first) * width : (end - first + 1) * width]
-                if known:
-                    acc[span(begin, end), :] += part
-                else:
-                    acc[span(begin, end), :] = part
-            seen.update(range(first, final + 1))
-
-        seen_c, seen_g = set(), set()
-        for lag in lags:
-            filt = gather_table(lag)
-            first, final = max(x_first, low_end - lag), min(high_end, conv_last - lag)
-            u_from, u_to = max(low_end, grad_first + lag), min(u_last, high_end + lag)
+    def filter_of(lag):
+        rows = []
+        for i in range(per_tile):
+            parts = []
+            for j in range(per_tile):
+                m = lag * per_tile + j - i
+                parts.append(table[m] if m >= 0 else jnp.zeros((block, block), jnp.bfloat16))
+            rows.append(jnp.concatenate(parts, axis=1))
+        return jnp.concatenate(rows, axis=0)
+
+    def add(acc, seen, first, final, value):
+        runs = []
+        for tile in range(first, final + 1):
+            if runs and runs[-1][2] == (tile in seen):
+                runs[-1][1] = tile
+            else:
+                runs.append([tile, tile, tile in seen])
+        for begin, end, known in runs:
+            part = value[(begin - first) * width : (end - first + 1) * width]
+            if known:
+                acc[span(begin, end), :] += part
+            else:
+                acc[span(begin, end), :] = part
+        seen.update(range(first, final + 1))
+
+    def convolve(g, x_tiles, out_tiles):
+        seen = set()
+        for lag in range(out_tiles[1] - x_tiles[0] + 1):
+            first = max(x_tiles[0], out_tiles[0] - lag)
+            final = min(x_tiles[1], out_tiles[1] - lag)
             if first <= final:
-                add(acc_c, seen_c, first + lag, final + lag, dot(xs[g, span(first, final), :], filt, NN))
-            if u_from <= u_to:
-                add(acc_g, seen_g, u_from - lag, u_to - lag, dot(us[g, span(u_from, u_to), :], filt, NT))
-
-        mine = span(low_end, high_end)
-        if which == 2:
-            part_out[g] = acc_c[last * layer_rows :, :].astype(jnp.bfloat16)
-            hand(g, 3).start()
-        if which == 1:
-            part_out[g] = acc_g[:layer_rows, :].astype(jnp.bfloat16)
-            hand(g, 0).start()
-        if which < last:
-            cv[g] = acc_c[mine, :].astype(jnp.bfloat16)
-            give_back(cv, conv_in, c_send, c_recv, g)
-        else:
-            held[g] = acc_c[mine, :]
-        if which > 0:
-            gv[g] = acc_g[mine, :].astype(jnp.bfloat16)
-            give_back(gv, gi_ref, g_send, g_recv, g)
-        else:
-            held[g] = acc_g[mine, :]
-
-        gram_first = 0 if inner else low_end
-        turned = dot(flip, xs[g, span(gram_first, high_end), :], NT).astype(jnp.bfloat16)
-
-        def window(first, count):
-            return us[g, first * width : (first + count) * width, :]
+                add(
+                    acc_c, seen, first + lag, final + lag,
+                    dot(xs[g, span(first, final), :], filter_of(lag), NN),
+                )
+
+    def correlate(g, u_tiles, out_tiles):
+        seen = set()
+        for lag in range(u_tiles[1] - out_tiles[0] + 1):
+            first = max(u_tiles[0], out_tiles[0] + lag)
+            final = min(u_tiles[1], out_tiles[1] + lag)
+            if first <= final:
+                add(
+                    acc_g, seen, first - lag, final - lag,
+                    dot(us[g, span(first, final), :], filter_of(lag), NT),
+                )
+
+    def filter_grad(g, x_tiles, u_tiles):
+        turned = {}
+
+        def turned_from(tile):
+            if tile not in turned:
+                rows = xs[g, span(tile, x_tiles[1]), :]
+                turned[tile] = dot(flip, rows, NT).astype(jnp.bfloat16)
+            return turned[tile]
 
         def gram_of(lag):
-            if not inner:
-                return dot(turned, window(low_end + lag, half), NN)
-            if which == 1:
-                return dot(turned, window(lag, 2 * half), NN)
-            if lag < SPLIT_LAG:
-                return dot(turned[:, 2 * half * width :], window(2 * half + lag, half), NN)
-            return dot(turned[:, : 2 * half * width], window(lag, 2 * half), NN)
-
-        gram_lags = half if not inner else (SPLIT_LAG if which == 1 else tiles)
+            first = max(x_tiles[0], u_tiles[0] - lag)
+            final = min(x_tiles[1], u_tiles[1] - lag)
+            base = x_tiles[0] + (first - x_tiles[0]) % per_tile
+            left = turned_from(base)[:, (first - base) * width : (final + 1 - base) * width]
+            return dot(left, us[g, span(first + lag, final + lag), :], NN)
+
+        lags = u_tiles[1] - x_tiles[0] + 1
         zero = jnp.zeros((block, block), jnp.float32)
         gram = gram_of(0)
         current = gram[block:, :block] + gram[:block, block:]
-        for lag in range(gram_lags):
-            following = gram_of(lag + 1) if lag + 1 < gram_lags else None
+        for lag in range(lags):
+            following = gram_of(lag + 1) if lag + 1 < lags else None
             odd = gram[block:, block:]
             if following is None:
                 even = zero
@@ -549,13 +600,71 @@
                 fg_out[lag * per_tile + i, pl.ds(g, 1), :] = total
             current, gram = even, following
 
+    def send_grads(g, which):
         @pl.when(g == groups - 1)
         def _():
             for to in grad_targets[which]:
                 grad_hop(which, to).start()
 
-    grad_targets = {0: (), 1: (0,), 2: (0, 1, 3), 3: (0,)}
-    grad_sources = {0: (1, 2, 3), 1: (2,), 2: (), 3: (2,)}
+    def back_conv(g, tile):
+        cv[g] = acc_c[span(tile, tile + half - 1), :].astype(jnp.bfloat16)
+        give_back(cv, conv_in, c_send, c_recv, g)
+
+    def back_grad(g, tile):
+        gv[g] = acc_g[span(tile, tile + half - 1), :].astype(jnp.bfloat16)
+        give_back(gv, gi_ref, g_send, g_recv, g)
+
+    def compute_for(which, g):
+        low, high = which * half, (which + 1) * half - 1
+
+        @pl.when(g == 0)
+        def _():
+            for origin in filt_sources[which]:
+                filt_hop(origin, which).wait_recv()
+            if which == 2:
+                pl.semaphore_wait(enter_sem.at[3], peers)
+                filt_hop(0, 3).start()
+            for origin in sorted(filt_sources[which] + ((which,) if which < last else ())):
+                filt_all[origin] = (
+                    filt_layer[origin].astype(jnp.float32).reshape(peers, groups, block)
+                )
+
+        make_table(g, half if which in (0, last) else tiles)
+        if which == 0:
+            convolve(g, (low, high), (low, high))
+            back_conv(g, low)
+        if which == 1:
+            wait_u(g)
+            hop_u(g, 0, 1).wait_recv()
+            convolve(g, (0, high), (low, high))
+            back_conv(g, low)
+            filter_grad(g, (0, high), (0, high))
+            send_grads(g, which)
+            hop_u(g, 2, 1).wait_recv()
+            hop_u(g, 3, 1).wait_recv()
+            correlate(g, (0, tiles - 1), (0, high))
+            far[g] = acc_g[span(0, low - 1), :].astype(jnp.bfloat16)
+            send_far(g, gi_ref, g_recv, 0)
+            back_grad(g, low)
+        if which == 2:
+            wait_x(g)
+            hop_x(g, 3, 2).wait_recv()
+            correlate(g, (low, tiles - 1), (low, high))
+            back_grad(g, low)
+            hop_x(g, 1, 2).wait_recv()
+            hop_x(g, 0, 2).wait_recv()
+            filter_grad(g, (0, tiles - 1), (low, tiles - 1))
+            send_grads(g, which)
+            convolve(g, (0, tiles - 1), (low, tiles - 1))
+            far[g] = acc_c[span(high + 1, tiles - 1), :].astype(jnp.bfloat16)
+            send_far(g, conv_in, c_recv, 3)
+            back_conv(g, low)
+        if which == 3:
+            correlate(g, (low, high), (low, high))
+            back_grad(g, low)
+
+    grad_targets = {0: (), 1: (0,), 2: (0, 1, 3), 3: ()}
+    grad_sources = {0: (1, 2), 1: (2,), 2: (), 3: (2,)}
 
     def grad_hop(origin, to_layer):
         return remote(
@@ -563,38 +672,31 @@
             fz_recv.at[origin], to_layer * peers + spot,
         )
 
-    def finish(g):
-        @pl.when(layer == last)
-        def _():
-            hand(g, last).wait_recv()
-            cv[g] = (held[g] + part_in[g].astype(jnp.float32)).astype(jnp.bfloat16)
-            give_back(cv, conv_in, c_send, c_recv, g)
-
-        @pl.when(layer == 0)
-        def _():
-            hand(g, 0).wait_recv()
-            gv[g] = (held[g] + part_in[g].astype(jnp.float32)).astype(jnp.bfloat16)
-            give_back(gv, gi_ref, g_send, g_recv, g)
-
     def stage(step, delay, body):
         @pl.when((step >= delay) & (step < groups + delay))
         def _():
             body(step - delay)
 
+    def scatter_later(g):
+        @pl.when(g >= LEAD)
+        def _():
+            scatter_both(g)
+
     def pipeline(step, carry):
         stage(step, 0, gather_layer)
+        stage(step, -LEAD, scatter_later)
+        stage(step, DELAY_RELAY, relay)
         stage(step, DELAY_COMPUTE, compute)
-        stage(step, DELAY_FINISH, finish)
         return carry
 
-    lax.fori_loop(0, groups + DELAY_FINISH, pipeline, 0)
+    lax.fori_loop(0, groups + DELAY_COMPUTE, pipeline, 0)
 
     for which in range(LAYERS):
 
         @pl.when(layer == which)
         def _(which=which):
             total = None
-            if which != 3:
+            if which in (1, 2):
                 total = fg_out[which * peers : (which + 1) * peers]
             for origin in grad_sources[which]:
                 grad_hop(origin, which).wait_recv()
@@ -626,21 +728,22 @@
     sent = pl.ds(0, groups * (peers - 1) // peers)
     wait_bytes(cv.at[sent], x_send.at[0])
     wait_bytes(cv.at[sent], u_send.at[0])
-    wait_bytes(cv.at[sent], c_send.at[0])
-    wait_bytes(cv.at[sent], g_send.at[0])
     wait_bytes(filt_in.at[pl.ds(0, crew - 1)], k_send.at[0])
     wait_bytes(filt_in.at[pl.ds(0, crew - 1)], f_send.at[2])
+    wait_bytes(cv, z_send.at[0])
+    wait_bytes(cv, z_send.at[0])
     for which in range(LAYERS):
 
         @pl.when(layer == which)
         def _(which=which):
-            hops = 1 if which in (1, 2) else 2
-            for _ in range(hops):
-                wait_bytes(cv, z_send.at[0])
+            if which < last:
+                wait_bytes(cv.at[sent], c_send.at[0])
+            if which > 0:
+                wait_bytes(cv.at[sent], g_send.at[0])
             if which in (1, 2):
-                wait_bytes(cv, p_send.at[0])
-            for _ in filt_targets[which]:
-                wait_bytes(filt_all.at[0], f_send.at[1])
+                wait_bytes(cv, far_send.at[0])
+            for _ in filt_targets[which] + ((3,) if which == 2 else ()):
+                wait_bytes(filt_layer.at[0], f_send.at[1])
             for _ in grad_targets[which]:
                 wait_bytes(fg_layer.at[0], f_send.at[0])
 
@@ -693,18 +796,17 @@
             pltpu.VMEM(filters.shape, jnp.float32),
             small,
             small,
+            pltpu.VMEM((LAYERS, peers // 2, 2 * groups, block), jnp.bfloat16),
             pltpu.VMEM((LAYERS, peers, groups, block), jnp.float32),
             flat,
             pltpu.VMEM((groups, rows, TILE), jnp.bfloat16),
-            pltpu.VMEM((groups, rows + 2 * layer_rows, TILE), jnp.bfloat16),
+            pltpu.VMEM((groups, rows, TILE), jnp.bfloat16),
             pltpu.VMEM((blocks, block, block), jnp.bfloat16),
             pltpu.VMEM((rows, TILE), jnp.float32),
             pltpu.VMEM((rows, TILE), jnp.float32),
             layered,
             layered,
             flat,
-            pltpu.VMEM((groups, layer_rows, TILE), jnp.float32),
-            layered,
             layered,
             pltpu.VMEM((blocks, groups, block), jnp.float32),
             pltpu.VMEM((LAYERS, peers, groups, block), jnp.float32),
@@ -724,11 +826,12 @@
             single,
             single,
             pltpu.SemaphoreType.DMA((groups, LAYERS)),
-            by_group,
+            pltpu.SemaphoreType.DMA((groups, LAYERS)),
             single,
             by_layer,
             single,
             by_layer,
+            pltpu.SemaphoreType.REGULAR((LAYERS,)),
         ],
         compiler_params=pltpu.CompilerParams(
             collective_id=0, has_side_effects=True, vmem_limit_bytes=VMEM_LIMIT
@@ -740,10 +843,11 @@
         in_specs=[vmem] * 3,
         out_specs=(hbm, hbm, hbm),
         scratch_shapes=[pltpu.SemaphoreType.DMA((3,))],
+        compiler_params=pltpu.CompilerParams(vmem_limit_bytes=1024 * 1024),
     )(*results)
 
 
-VMEM_LIMIT = 56 * 1024 * 1024
+VMEM_LIMIT = 53900 * 1024
 
 
 def solution(mesh):

time: 47.6 us -> 44.5 us (0.935)
  Pallas kernels: 46.8 us -> 42.9 us
  local copies, waits for them, and re-layouts: 0 us -> 0.75 us
    pallas_call x1, Pallas kernels: 44.6 us -> 41.9 us  [layered_shards(): pl.pallas_call(functools.partial(layered_kernel, seq_count, chan_count),...]
    pallas_call x1, Pallas kernels: 2.2 us -> 1 us  [layered_shards(): pl.pallas_call(store_kernel, out_shape=outs, in_specs=[vmem] * 3, out_spe...]
    unnamed x0 -> x2, local copies, waits for them, and re-layouts: none -> 0.75 us
where the time goes in v2:
time: 44.5 us; the launch traced here: 44.3 us
  Pallas kernels  42.9 us (96%)
  local copies, waits for them, and re-layouts  0.75 us (2%)
  between operations  0.65 us (1%)
    pallas_call x1, Pallas kernels, layered_shards(): pl.pallas_call(functools.partial(layered_kernel, seq_count, chan_count),...  41.9 us
    pallas_call x1, Pallas kernels, layered_shards(): pl.pallas_call(store_kernel, out_shape=outs, in_specs=[vmem] * 3, out_spe...  1 us

profile of v2, /device:TPU:0, one launch (start us, length us, event | category | flops | bytes accessed | tf_op | source)
XLA Modules:
  0.0 44.3 jit_solution(5056693560853977438)
XLA Ops:
  0.6 0.0 copy-start
  0.6 0.7 %copy-done = f32[64,64]{1,0:T(8,128)S(1)} copy-done((f32[64,64]{1,0:T(8,128)S(1)}, f32[64,64]{1,0:T(8,128)}, u32[]{:S(2)}) %copy-start) | copy-done | bytes 16408
  1.4 41.9 %shard_map.67 = (bf16[2048,128]{1,0:T(8,128)(2,1)S(1)}, bf16[2048,128]{1,0:T(8,128)(2,1)S(1)}, f32[64,64]{1,0:T(8,128)S(1)}) custom-call(bf16[2048,128]{1,0:T(8,128)(2,1)} %x_hbm.1, bf16[2048,128]{1,0:T(8,128)(2,1)} %gate_hbm.1, bf16[2048,128]{1,0:T(8,128)(2,1)} %up_hbm.1, f32[64,64]{1,0:T(8,128)S(1)} %copy-done), custom_call_target="tpu_custom_call" | custom-call | tf_op jit(solution)/shard_map/pallas_call | solution.py:788
  43.3 1.0 %shard_map.68 = (bf16[2048,128]{1,0:T(8,128)(2,1)}, bf16[2048,128]{1,0:T(8,128)(2,1)}, f32[64,64]{1,0:T(8,128)}) custom-call(bf16[2048,128]{1,0:T(8,128)(2,1)S(1)} %get-tuple-element.6.a_ref, bf16[2048,128]{1,0:T(8,128)(2,1)S(1)} %get-tuple-element.7.b_ref, f32[64,64]{1,0:T(8,128)S(1)} %get-tuple-element.8.c_ref), custom_call_target="tpu_custom_call" | custom-call | tf_op jit(solution)/shard_map/pallas_call | solution.py:840
Async XLA Ops:
  0.6 0.8 %copy-start = (f32[64,64]{1,0:T(8,128)S(1)}, f32[64,64]{1,0:T(8,128)}, u32[]{:S(2)}) copy-start(f32[64,64]{1,0:T(8,128)} %raw_hbm.1) | copy-start | bytes 49156

commit v3 on v2

--- a/solution.py
+++ b/solution.py
@@ -146,7 +146,7 @@
 MESH = pl.DeviceIdType.MESH
 TILE = 256
 LAYERS = 4
-LEAD, DELAY_RELAY, DELAY_COMPUTE = 4, 2, 3
+LEAD, DELAY_SECOND, DELAY_RELAY, DELAY_COMPUTE, DELAY_OUTER = 4, 1, 2, 3, 6
 NT = (((1,), (1,)), ((), ()))
 NN = (((1,), (0,)), ((), ()))
 
@@ -262,6 +262,7 @@
                 for p in spots:
                     greet(to_layer * peers + p, chan)
 
+    fg_out[...] = jnp.zeros_like(fg_out)
     loads[2].wait()
     scaled = raw_ref[...] * factor
     lanes = jnp.concatenate([scaled] * chan_count, axis=1)
@@ -293,6 +294,7 @@
     def _():
         for p in everyone:
             enter(3, 2, p)
+        enter(3, 1, spot)
 
     def place(ref, g, s):
         return ref.at[
@@ -328,15 +330,18 @@
             ).start()
         pltpu.make_async_copy(strip(ref, spot, g), place(buf, g, seq), recv.at[g]).start()
 
+    def mirror(g):
+        return groups - 1 - g
+
     def scatter_both(g):
         @pl.when(layer < LAYERS // 2)
         def _():
             scatter(x_hbm, xs, x_send, x_recv, g)
-            scatter(u_loc, us, u_send, u_recv, g)
+            scatter(u_loc, us, u_send, u_recv, mirror(g))
 
         @pl.when(layer >= LAYERS // 2)
         def _():
-            scatter(u_loc, us, u_send, u_recv, g)
+            scatter(u_loc, us, u_send, u_recv, mirror(g))
             scatter(x_hbm, xs, x_send, x_recv, g)
 
     def give_back(buf, ref, send, recv, g):
@@ -363,8 +368,9 @@
         ref = layer_span(us, g, origin)
         return remote(ref, ref, z_send.at[0], zu_recv.at[g, origin], to_layer * peers + spot)
 
-    def ahead(from_ref, buf, recv, origin, to_layer):
-        def step(g, carry):
+    def ahead(from_ref, buf, recv, origin, to_layer, order=lambda g: g):
+        def step(i, carry):
+            g = order(i)
             remote(
                 strip(from_ref, spot, g), place(buf, g, seq), z_send.at[0], recv.at[g, origin],
                 to_layer * peers + spot,
@@ -397,11 +403,11 @@
 
     @pl.when(layer == 2)
     def _():
-        ahead(u_loc, us, zu_recv, 2, 1)
+        ahead(u_loc, us, zu_recv, 2, 1, mirror)
 
     @pl.when(layer == 3)
     def _():
-        ahead(u_loc, us, zu_recv, 3, 2)
+        ahead(u_loc, us, zu_recv, 3, 2, mirror)
 
     for k in range(1, crew):
         p, c = crew_member(k)
@@ -455,8 +461,6 @@
         def _():
             wait_x(g)
             rest(g, xs, zx_recv, 0, 1)
-            wait_u(g)
-            hop_u(g, 0, 1).start()
 
         @pl.when(layer == 1)
         def _():
@@ -465,20 +469,29 @@
 
         @pl.when(layer == 2)
         def _():
-            wait_u(g)
-            rest(g, us, zu_recv, 2, 1)
+            wait_u(mirror(g))
+            rest(mirror(g), us, zu_recv, 2, 1)
 
         @pl.when(layer == 3)
         def _():
-            wait_u(g)
-            rest(g, us, zu_recv, 3, 2)
+            wait_u(mirror(g))
+            rest(mirror(g), us, zu_recv, 3, 2)
+
+        @pl.when(g == 0)
+        def _():
+            spread_filters()
+
+    def second(g):
+        @pl.when(layer == 0)
+        def _():
+            wait_u(mirror(g))
+            hop_u(mirror(g), 0, 1).start()
+
+        @pl.when(layer == 3)
+        def _():
             wait_x(g)
             hop_x(g, 3, 2).start()
 
-        @pl.when(g == 0)
-        def _():
-            spread_filters()
-
     def relay(g):
         @pl.when(layer == 1)
         def _():
@@ -487,8 +500,8 @@
 
         @pl.when(layer == 2)
         def _():
-            hop_u(g, 3, 2).wait_recv()
-            hop_u(g, 3, 1).start()
+            hop_u(mirror(g), 3, 2).wait_recv()
+            hop_u(mirror(g), 3, 1).start()
 
     row_id = lax.broadcasted_iota(jnp.int32, (TILE, TILE), 0)
     col_id = lax.broadcasted_iota(jnp.int32, (TILE, TILE), 1)
@@ -498,8 +511,8 @@
     upper = col_in >= row_in
     lower_flipped = col_in + row_in >= block - 1
 
-    def compute(g):
-        for which in range(LAYERS):
+    def compute(g, layers):
+        for which in layers:
 
             @pl.when(layer == which)
             def _(which=which):
@@ -603,6 +616,8 @@
     def send_grads(g, which):
         @pl.when(g == groups - 1)
         def _():
+            if which == 1:
+                pl.semaphore_wait(enter_sem.at[3], 1)
             for to in grad_targets[which]:
                 grad_hop(which, to).start()
 
@@ -629,42 +644,58 @@
                     filt_layer[origin].astype(jnp.float32).reshape(peers, groups, block)
                 )
 
-        make_table(g, half if which in (0, last) else tiles)
+        other = mirror(g)
         if which == 0:
+            make_table(g, half)
             convolve(g, (low, high), (low, high))
             back_conv(g, low)
         if which == 1:
-            wait_u(g)
-            hop_u(g, 0, 1).wait_recv()
+            make_table(g, 2 * half)
             convolve(g, (0, high), (low, high))
             back_conv(g, low)
-            filter_grad(g, (0, high), (0, high))
+            wait_u(other)
+            hop_u(other, 0, 1).wait_recv()
+
+            @pl.when(g >= groups // 2)
+            def _():
+                filter_grad(g, (0, high), (0, tiles - 1))
+                filter_grad(other, (0, high), (0, high))
+
             send_grads(g, which)
-            hop_u(g, 2, 1).wait_recv()
-            hop_u(g, 3, 1).wait_recv()
-            correlate(g, (0, tiles - 1), (0, high))
-            far[g] = acc_g[span(0, low - 1), :].astype(jnp.bfloat16)
-            send_far(g, gi_ref, g_recv, 0)
-            back_grad(g, low)
+            make_table(other, tiles)
+            hop_u(other, 2, 1).wait_recv()
+            hop_u(other, 3, 1).wait_recv()
+            correlate(other, (0, tiles - 1), (0, high))
+            far[other] = acc_g[span(0, low - 1), :].astype(jnp.bfloat16)
+            send_far(other, gi_ref, g_recv, 0)
+            back_grad(other, low)
         if which == 2:
+            make_table(other, 2 * half)
+            correlate(other, (low, tiles - 1), (low, high))
+            back_grad(other, low)
             wait_x(g)
             hop_x(g, 3, 2).wait_recv()
-            correlate(g, (low, tiles - 1), (low, high))
-            back_grad(g, low)
+
+            @pl.when(g >= groups // 2)
+            def _():
+                filter_grad(other, (0, tiles - 1), (low, tiles - 1))
+                filter_grad(g, (low, tiles - 1), (low, tiles - 1))
+
+            send_grads(g, which)
+            make_table(g, tiles)
             hop_x(g, 1, 2).wait_recv()
             hop_x(g, 0, 2).wait_recv()
-            filter_grad(g, (0, tiles - 1), (low, tiles - 1))
-            send_grads(g, which)
             convolve(g, (0, tiles - 1), (low, tiles - 1))
             far[g] = acc_c[span(high + 1, tiles - 1), :].astype(jnp.bfloat16)
             send_far(g, conv_in, c_recv, 3)
             back_conv(g, low)
         if which == 3:
-            correlate(g, (low, high), (low, high))
-            back_grad(g, low)
-
-    grad_targets = {0: (), 1: (0,), 2: (0, 1, 3), 3: ()}
-    grad_sources = {0: (1, 2), 1: (2,), 2: (), 3: (2,)}
+            make_table(other, half)
+            correlate(other, (low, high), (low, high))
+            back_grad(other, low)
+
+    grad_targets = {0: (), 1: (0, 2, 3), 2: (0, 1, 3), 3: ()}
+    grad_sources = {0: (1, 2), 1: (2,), 2: (1,), 3: (1, 2)}
 
     def grad_hop(origin, to_layer):
         return remote(
@@ -685,11 +716,13 @@
     def pipeline(step, carry):
         stage(step, 0, gather_layer)
         stage(step, -LEAD, scatter_later)
+        stage(step, DELAY_SECOND, second)
         stage(step, DELAY_RELAY, relay)
-        stage(step, DELAY_COMPUTE, compute)
+        stage(step, DELAY_COMPUTE, lambda g: compute(g, (1, 2)))
+        stage(step, DELAY_OUTER, lambda g: compute(g, (0, last)))
         return carry
 
-    lax.fori_loop(0, groups + DELAY_COMPUTE, pipeline, 0)
+    lax.fori_loop(0, groups + DELAY_OUTER, pipeline, 0)
 
     for which in range(LAYERS):
 

time: 44.5 us -> 43.4 us (0.975)
  Pallas kernels: 42.9 us -> 41.8 us
    pallas_call x1, Pallas kernels: 41.9 us -> 40.8 us  [layered_shards(): pl.pallas_call(functools.partial(layered_kernel, seq_count, chan_count),...]
where the time goes in v3:
time: 43.4 us; the launch traced here: 43.2 us
  Pallas kernels  41.8 us (96%)
  local copies, waits for them, and re-layouts  0.75 us (2%)
  between operations  0.65 us (1%)
    pallas_call x1, Pallas kernels, layered_shards(): pl.pallas_call(functools.partial(layered_kernel, seq_count, chan_count),...  40.8 us
    pallas_call x1, Pallas kernels, layered_shards(): pl.pallas_call(store_kernel, out_shape=outs, in_specs=[vmem] * 3, out_spe...  1 us

profile of v3, /device:TPU:0, one launch (start us, length us, event | category | flops | bytes accessed | tf_op | source)
XLA Modules:
  0.0 43.2 jit_solution(17069649744278784789)
XLA Ops:
  0.6 0.0 copy-start
  0.6 0.7 %copy-done = f32[64,64]{1,0:T(8,128)S(1)} copy-done((f32[64,64]{1,0:T(8,128)S(1)}, f32[64,64]{1,0:T(8,128)}, u32[]{:S(2)}) %copy-start) | copy-done | bytes 16408
  1.4 40.8 %shard_map.67 = (bf16[2048,128]{1,0:T(8,128)(2,1)S(1)}, bf16[2048,128]{1,0:T(8,128)(2,1)S(1)}, f32[64,64]{1,0:T(8,128)S(1)}) custom-call(bf16[2048,128]{1,0:T(8,128)(2,1)} %x_hbm.1, bf16[2048,128]{1,0:T(8,128)(2,1)} %gate_hbm.1, bf16[2048,128]{1,0:T(8,128)(2,1)} %up_hbm.1, f32[64,64]{1,0:T(8,128)S(1)} %copy-done), custom_call_target="tpu_custom_call" | custom-call | tf_op jit(solution)/shard_map/pallas_call | solution.py:821
  42.2 1.0 %shard_map.68 = (bf16[2048,128]{1,0:T(8,128)(2,1)}, bf16[2048,128]{1,0:T(8,128)(2,1)}, f32[64,64]{1,0:T(8,128)}) custom-call(bf16[2048,128]{1,0:T(8,128)(2,1)S(1)} %get-tuple-element.6.a_ref, bf16[2048,128]{1,0:T(8,128)(2,1)S(1)} %get-tuple-element.7.b_ref, f32[64,64]{1,0:T(8,128)S(1)} %get-tuple-element.8.c_ref), custom_call_target="tpu_custom_call" | custom-call | tf_op jit(solution)/shard_map/pallas_call | solution.py:873
Async XLA Ops:
  0.6 0.8 %copy-start = (f32[64,64]{1,0:T(8,128)S(1)}, f32[64,64]{1,0:T(8,128)}, u32[]{:S(2)}) copy-start(f32[64,64]{1,0:T(8,128)} %raw_hbm.1) | copy-start | bytes 49156

commit v4 on v3

--- a/solution.py
+++ b/solution.py
@@ -183,8 +183,6 @@
     conv_in,
     far,
     fg_out,
-    fg_layer,
-    fg_sum,
     fg_in,
     load_sem,
     x_send,
@@ -202,7 +200,6 @@
     zx_recv,
     zu_recv,
     f_recv,
-    fz_recv,
     k_recv,
     kz_recv,
     enter_sem,
@@ -247,11 +244,12 @@
     for k in range(1, crew):
         p, c = crew_member(k)
         greet(layer * peers + p, c)
-    everyone, lone = range(peers), (spot,)
+    everyone = [(p, c) for p in range(peers) for c in range(chan_count)]
+    lone = [(spot, chan)]
     greeted = {
-        0: ((1, everyone), (2, lone)),
-        1: ((0, lone), (2, lone), (3, lone)),
-        2: ((0, lone), (1, lone), (3, everyone)),
+        0: ((1, everyone), (2, everyone)),
+        1: ((0, lone), (2, everyone), (3, everyone)),
+        2: ((0, lone), (1, everyone), (3, everyone)),
         3: (),
     }
     for which in range(LAYERS):
@@ -259,8 +257,8 @@
         @pl.when(layer == which)
         def _(which=which):
             for to_layer, spots in greeted[which]:
-                for p in spots:
-                    greet(to_layer * peers + p, chan)
+                for p, c in spots:
+                    greet(to_layer * peers + p, c)
 
     fg_out[...] = jnp.zeros_like(fg_out)
     loads[2].wait()
@@ -275,26 +273,26 @@
     u_loc[...] = (
         gate_ref[...].astype(jnp.float32) * up_ref[...].astype(jnp.float32)
     ).astype(jnp.bfloat16)
-    expected = {0: 2, 1: peers + 1, 2: 2, 3: 1 + peers}
+    expected = {0: 2, 1: 2 * crew, 2: 2 * crew, 3: 2 * crew}
     for which in range(LAYERS):
 
         @pl.when(layer == which)
         def _(which=which):
             pl.semaphore_wait(barrier, crew - 1 + expected[which])
 
-    def enter(origin, to_layer, p):
+    def enter(origin, to_layer, p, c):
         pl.semaphore_signal(
             enter_sem.at[origin],
             inc=1,
-            device_id=(to_layer * peers + p, chan),
+            device_id=(to_layer * peers + p, c),
             device_id_type=MESH,
         )
 
     @pl.when(layer == 3)
     def _():
-        for p in everyone:
-            enter(3, 2, p)
-        enter(3, 1, spot)
+        for p, c in everyone:
+            enter(3, 2, p, c)
+            enter(3, 1, p, c)
 
     def place(ref, g, s):
         return ref.at[
@@ -331,7 +329,7 @@
         pltpu.make_async_copy(strip(ref, spot, g), place(buf, g, seq), recv.at[g]).start()
 
     def mirror(g):
-        return groups - 1 - g
+        return g + 1 - 2 * lax.rem(g, 2)
 
     def scatter_both(g):
         @pl.when(layer < LAYERS // 2)
@@ -617,9 +615,18 @@
         @pl.when(g == groups - 1)
         def _():
             if which == 1:
-                pl.semaphore_wait(enter_sem.at[3], 1)
-            for to in grad_targets[which]:
-                grad_hop(which, to).start()
+                pl.semaphore_wait(enter_sem.at[3], crew)
+            for to in range(LAYERS):
+                for k in range(1 if to == which else 0, crew):
+                    p, c = crew_member(k)
+                    remote(
+                        fg_out.at[to * peers + p], fg_in.at[which, chan * peers + spot],
+                        f_send.at[0], f_recv.at[which], to * peers + p, c,
+                    ).start()
+            pltpu.make_async_copy(
+                fg_out.at[which * peers + spot], fg_in.at[which, chan * peers + spot],
+                f_recv.at[which],
+            ).start()
 
     def back_conv(g, tile):
         cv[g] = acc_c[span(tile, tile + half - 1), :].astype(jnp.bfloat16)
@@ -637,7 +644,7 @@
             for origin in filt_sources[which]:
                 filt_hop(origin, which).wait_recv()
             if which == 2:
-                pl.semaphore_wait(enter_sem.at[3], peers)
+                pl.semaphore_wait(enter_sem.at[3], crew)
                 filt_hop(0, 3).start()
             for origin in sorted(filt_sources[which] + ((which,) if which < last else ())):
                 filt_all[origin] = (
@@ -645,6 +652,9 @@
                 )
 
         other = mirror(g)
+        odd = lax.rem(g, 2) == 1
+        final = g == groups - 1
+        own_step = (jnp.logical_not(odd) & (g > 0)) | final
         if which == 0:
             make_table(g, half)
             convolve(g, (low, high), (low, high))
@@ -656,10 +666,13 @@
             wait_u(other)
             hop_u(other, 0, 1).wait_recv()
 
-            @pl.when(g >= groups // 2)
+            @pl.when(odd)
             def _():
                 filter_grad(g, (0, high), (0, tiles - 1))
-                filter_grad(other, (0, high), (0, high))
+
+            @pl.when(own_step)
+            def _():
+                filter_grad(g - 2 + g // (groups - 1), (0, high), (0, high))
 
             send_grads(g, which)
             make_table(other, tiles)
@@ -676,10 +689,13 @@
             wait_x(g)
             hop_x(g, 3, 2).wait_recv()
 
-            @pl.when(g >= groups // 2)
+            @pl.when(odd)
             def _():
                 filter_grad(other, (0, tiles - 1), (low, tiles - 1))
-                filter_grad(g, (low, tiles - 1), (low, tiles - 1))
+
+            @pl.when(own_step)
+            def _():
+                filter_grad(g - 1 + g // (groups - 1), (low, tiles - 1), (low, tiles - 1))
 
             send_grads(g, which)
             make_table(g, tiles)
@@ -694,15 +710,6 @@
             correlate(other, (low, high), (low, high))
             back_grad(other, low)
 
-    grad_targets = {0: (), 1: (0, 2, 3), 2: (0, 1, 3), 3: ()}
-    grad_sources = {0: (1, 2), 1: (2,), 2: (1,), 3: (1, 2)}
-
-    def grad_hop(origin, to_layer):
-        return remote(
-            fg_out.at[pl.ds(to_layer * peers, peers)], fg_layer.at[origin], f_send.at[0],
-            fz_recv.at[origin], to_layer * peers + spot,
-        )
-
     def stage(step, delay, body):
         @pl.when((step >= delay) & (step < groups + delay))
         def _():
@@ -724,35 +731,15 @@
 
     lax.fori_loop(0, groups + DELAY_OUTER, pipeline, 0)
 
-    for which in range(LAYERS):
-
-        @pl.when(layer == which)
-        def _(which=which):
-            total = None
-            if which in (1, 2):
-                total = fg_out[which * peers : (which + 1) * peers]
-            for origin in grad_sources[which]:
-                grad_hop(origin, which).wait_recv()
-                part = fg_layer[origin]
-                total = part if total is None else total + part
-            fg_sum[...] = total
-
-    for k in range(1, crew):
-        p, c = crew_member(k)
-        remote(
-            fg_sum.at[p], fg_in.at[chan * peers + spot], f_send.at[2], f_recv.at[0],
-            layer * peers + p, c,
-        ).start()
-    pltpu.make_async_copy(fg_sum.at[spot], fg_in.at[chan * peers + spot], f_recv.at[0]).start()
-
     wait_bytes(conv_in, c_recv.at[0])
     gg_ref[...] = (up_ref[...].astype(jnp.float32) * conv_in[...].astype(jnp.float32)).astype(
         jnp.bfloat16
     )
     wait_bytes(gi_ref, g_recv.at[0])
-    wait_bytes(fg_in, f_recv.at[0])
+    wait_bytes(fg_in.at[1], f_recv.at[1])
+    wait_bytes(fg_in.at[2], f_recv.at[2])
     for i in range(crew):
-        total = fg_in[i]
+        total = fg_in[1, i] + fg_in[2, i]
         kept_part = total[:, :share]
         for d in range(1, chan_count):
             kept_part = jnp.where(chan == d, total[:, d * share : (d + 1) * share], kept_part)
@@ -762,7 +749,6 @@
     wait_bytes(cv.at[sent], x_send.at[0])
     wait_bytes(cv.at[sent], u_send.at[0])
     wait_bytes(filt_in.at[pl.ds(0, crew - 1)], k_send.at[0])
-    wait_bytes(filt_in.at[pl.ds(0, crew - 1)], f_send.at[2])
     wait_bytes(cv, z_send.at[0])
     wait_bytes(cv, z_send.at[0])
     for which in range(LAYERS):
@@ -777,8 +763,10 @@
                 wait_bytes(cv, far_send.at[0])
             for _ in filt_targets[which] + ((3,) if which == 2 else ()):
                 wait_bytes(filt_layer.at[0], f_send.at[1])
-            for _ in grad_targets[which]:
-                wait_bytes(fg_layer.at[0], f_send.at[0])
+            if which in (1, 2):
+                for _ in range(LAYERS - 1):
+                    wait_bytes(fg_in.at[0], f_send.at[0])
+                wait_bytes(fg_in.at[0, pl.ds(0, crew - 1)], f_send.at[0])
 
 
 def store_kernel(a_ref, b_ref, c_ref, a_out, b_out, c_out, sems):
@@ -842,9 +830,7 @@
             flat,
             layered,
             pltpu.VMEM((blocks, groups, block), jnp.float32),
-            pltpu.VMEM((LAYERS, peers, groups, block), jnp.float32),
-            pltpu.VMEM((peers, groups, block), jnp.float32),
-            small,
+            pltpu.VMEM((LAYERS, crew, groups, block), jnp.float32),
             pltpu.SemaphoreType.DMA((3,)),
             single,
             single,
@@ -860,7 +846,6 @@
             single,
             pltpu.SemaphoreType.DMA((groups, LAYERS)),
             pltpu.SemaphoreType.DMA((groups, LAYERS)),
-            single,
             by_layer,
             single,
             by_layer,

time: 43.4 us -> 41.4 us (0.954)
  Pallas kernels: 41.8 us -> 39.8 us
    pallas_call x1, Pallas kernels: 40.8 us -> 38.8 us  [layered_shards(): pl.pallas_call(functools.partial(layered_kernel, seq_count, chan_count),...]
where the time goes in v4:
time: 41.4 us; the launch traced here: 41.2 us
  Pallas kernels  39.8 us (96%)
  local copies, waits for them, and re-layouts  0.75 us (2%)
  between operations  0.65 us (2%)
    pallas_call x1, Pallas kernels, layered_shards(): pl.pallas_call(functools.partial(layered_kernel, seq_count, chan_count),...  38.8 us
    pallas_call x1, Pallas kernels, layered_shards(): pl.pallas_call(store_kernel, out_shape=outs, in_specs=[vmem] * 3, out_spe...  1 us

profile of v4, /device:TPU:0, one launch (start us, length us, event | category | flops | bytes accessed | tf_op | source)
XLA Modules:
  0.0 41.2 jit_solution(11087208392263443517)
XLA Ops:
  0.6 0.0 copy-start
  0.6 0.7 %copy-done = f32[64,64]{1,0:T(8,128)S(1)} copy-done((f32[64,64]{1,0:T(8,128)S(1)}, f32[64,64]{1,0:T(8,128)}, u32[]{:S(2)}) %copy-start) | copy-done | bytes 16408
  1.4 38.8 %shard_map.67 = (bf16[2048,128]{1,0:T(8,128)(2,1)S(1)}, bf16[2048,128]{1,0:T(8,128)(2,1)S(1)}, f32[64,64]{1,0:T(8,128)S(1)}) custom-call(bf16[2048,128]{1,0:T(8,128)(2,1)} %x_hbm.1, bf16[2048,128]{1,0:T(8,128)(2,1)} %gate_hbm.1, bf16[2048,128]{1,0:T(8,128)(2,1)} %up_hbm.1, f32[64,64]{1,0:T(8,128)S(1)} %copy-done), custom_call_target="tpu_custom_call" | custom-call | tf_op jit(solution)/shard_map/pallas_call | solution.py:809
  40.2 1.0 %shard_map.68 = (bf16[2048,128]{1,0:T(8,128)(2,1)}, bf16[2048,128]{1,0:T(8,128)(2,1)}, f32[64,64]{1,0:T(8,128)}) custom-call(bf16[2048,128]{1,0:T(8,128)(2,1)S(1)} %get-tuple-element.6.a_ref, bf16[2048,128]{1,0:T(8,128)(2,1)S(1)} %get-tuple-element.7.b_ref, f32[64,64]{1,0:T(8,128)S(1)} %get-tuple-element.8.c_ref), custom_call_target="tpu_custom_call" | custom-call | tf_op jit(solution)/shard_map/pallas_call | solution.py:858
Async XLA Ops:
  0.6 0.8 %copy-start = (f32[64,64]{1,0:T(8,128)S(1)}, f32[64,64]{1,0:T(8,128)}, u32[]{:S(2)}) copy-start(f32[64,64]{1,0:T(8,128)} %raw_hbm.1) | copy-start | bytes 49156

commit v5 on v4

--- a/solution.py
+++ b/solution.py
@@ -390,23 +390,6 @@
             ).start()
 
     scatter_both(0)
-
-    @pl.when(layer == 0)
-    def _():
-        ahead(x_hbm, xs, zx_recv, 0, 1)
-
-    @pl.when(layer == 1)
-    def _():
-        ahead(x_hbm, xs, zx_recv, 1, 2)
-
-    @pl.when(layer == 2)
-    def _():
-        ahead(u_loc, us, zu_recv, 2, 1, mirror)
-
-    @pl.when(layer == 3)
-    def _():
-        ahead(u_loc, us, zu_recv, 3, 2, mirror)
-
     for k in range(1, crew):
         p, c = crew_member(k)
         remote(
@@ -414,6 +397,23 @@
             layer * peers + p, c,
         ).start()
     pltpu.make_async_copy(filt_ref.at[chan * peers + spot], filt_in.at[slot], k_recv.at[0]).start()
+
+
+    @pl.when(layer == 0)
+    def _():
+        ahead(x_hbm, xs, zx_recv, 0, 1)
+
+    @pl.when(layer == 1)
+    def _():
+        ahead(x_hbm, xs, zx_recv, 1, 2)
+
+    @pl.when(layer == 2)
+    def _():
+        ahead(u_loc, us, zu_recv, 2, 1, mirror)
+
+    @pl.when(layer == 3)
+    def _():
+        ahead(u_loc, us, zu_recv, 3, 2, mirror)
 
     def scatter_early(g, carry):
         scatter_both(g)

time: 41.4 us -> 41.4 us (level)
  no operation moved by 1% of the time
where the time goes in v5:
time: 41.4 us; the launch traced here: 41.2 us
  Pallas kernels  39.8 us (96%)
  local copies, waits for them, and re-layouts  0.75 us (2%)
  between operations  0.65 us (2%)
    pallas_call x1, Pallas kernels, layered_shards(): pl.pallas_call(functools.partial(layered_kernel, seq_count, chan_count),...  38.8 us
    pallas_call x1, Pallas kernels, layered_shards(): pl.pallas_call(store_kernel, out_shape=outs, in_specs=[vmem] * 3, out_spe...  1 us

profile of v5, /device:TPU:0, one launch (start us, length us, event | category | flops | bytes accessed | tf_op | source)
XLA Modules:
  0.0 41.2 jit_solution(13985950854247694257)
XLA Ops:
  0.6 0.0 copy-start
  0.6 0.7 %copy-done = f32[64,64]{1,0:T(8,128)S(1)} copy-done((f32[64,64]{1,0:T(8,128)S(1)}, f32[64,64]{1,0:T(8,128)}, u32[]{:S(2)}) %copy-start) | copy-done | bytes 16408
  1.4 38.8 %shard_map.67 = (bf16[2048,128]{1,0:T(8,128)(2,1)S(1)}, bf16[2048,128]{1,0:T(8,128)(2,1)S(1)}, f32[64,64]{1,0:T(8,128)S(1)}) custom-call(bf16[2048,128]{1,0:T(8,128)(2,1)} %x_hbm.1, bf16[2048,128]{1,0:T(8,128)(2,1)} %gate_hbm.1, bf16[2048,128]{1,0:T(8,128)(2,1)} %up_hbm.1, f32[64,64]{1,0:T(8,128)S(1)} %copy-done), custom_call_target="tpu_custom_call" | custom-call | tf_op jit(solution)/shard_map/pallas_call | solution.py:809
  40.2 1.0 %shard_map.68 = (bf16[2048,128]{1,0:T(8,128)(2,1)}, bf16[2048,128]{1,0:T(8,128)(2,1)}, f32[64,64]{1,0:T(8,128)}) custom-call(bf16[2048,128]{1,0:T(8,128)(2,1)S(1)} %get-tuple-element.6.a_ref, bf16[2048,128]{1,0:T(8,128)(2,1)S(1)} %get-tuple-element.7.b_ref, f32[64,64]{1,0:T(8,128)S(1)} %get-tuple-element.8.c_ref), custom_call_target="tpu_custom_call" | custom-call | tf_op jit(solution)/shard_map/pallas_call | solution.py:858
Async XLA Ops:
  0.6 0.8 %copy-start = (f32[64,64]{1,0:T(8,128)S(1)}, f32[64,64]{1,0:T(8,128)}, u32[]{:S(2)}) copy-start(f32[64,64]{1,0:T(8,128)} %raw_hbm.1) | copy-start | bytes 49156

commit v6 on v4

--- a/solution.py
+++ b/solution.py
@@ -146,7 +146,7 @@
 MESH = pl.DeviceIdType.MESH
 TILE = 256
 LAYERS = 4
-LEAD, DELAY_SECOND, DELAY_RELAY, DELAY_COMPUTE, DELAY_OUTER = 4, 1, 2, 3, 6
+LEAD, DELAY_SECOND, DELAY_RELAY, DELAY_COMPUTE, DELAY_OUTER = 6, 1, 2, 3, 6
 NT = (((1,), (1,)), ((), ()))
 NN = (((1,), (0,)), ((), ()))
 
@@ -351,8 +351,7 @@
         pltpu.make_async_copy(place(buf, g, spot), strip(ref, spot, g), recv.at[0]).start()
 
     def send_far(g, ref, recv, to_layer):
-        for k in (2, 3, 1, 0):
-            p = lax.rem(spot + k, peers)
+        for p in range(peers):
             remote(
                 place(far, g, p), strip(ref, spot, g), far_send.at[0], recv.at[0],
                 to_layer * peers + p,

time: 41.4 us -> 41.4 us (level)
  no operation moved by 1% of the time
where the time goes in v6:
time: 41.4 us; the launch traced here: 41.2 us
  Pallas kernels  39.8 us (96%)
  local copies, waits for them, and re-layouts  0.75 us (2%)
  between operations  0.65 us (2%)
    pallas_call x1, Pallas kernels, layered_shards(): pl.pallas_call(functools.partial(layered_kernel, seq_count, chan_count),...  38.8 us
    pallas_call x1, Pallas kernels, layered_shards(): pl.pallas_call(store_kernel, out_shape=outs, in_specs=[vmem] * 3, out_spe...  1 us

profile of v6, /device:TPU:0, one launch (start us, length us, event | category | flops | bytes accessed | tf_op | source)
XLA Modules:
  0.0 41.2 jit_solution(15185883423534306892)
XLA Ops:
  0.6 0.0 copy-start
  0.6 0.7 %copy-done = f32[64,64]{1,0:T(8,128)S(1)} copy-done((f32[64,64]{1,0:T(8,128)S(1)}, f32[64,64]{1,0:T(8,128)}, u32[]{:S(2)}) %copy-start) | copy-done | bytes 16408
  1.4 38.8 %shard_map.67 = (bf16[2048,128]{1,0:T(8,128)(2,1)S(1)}, bf16[2048,128]{1,0:T(8,128)(2,1)S(1)}, f32[64,64]{1,0:T(8,128)S(1)}) custom-call(bf16[2048,128]{1,0:T(8,128)(2,1)} %x_hbm.1, bf16[2048,128]{1,0:T(8,128)(2,1)} %gate_hbm.1, bf16[2048,128]{1,0:T(8,128)(2,1)} %up_hbm.1, f32[64,64]{1,0:T(8,128)S(1)} %copy-done), custom_call_target="tpu_custom_call" | custom-call | tf_op jit(solution)/shard_map/pallas_call | solution.py:808
  40.2 1.0 %shard_map.68 = (bf16[2048,128]{1,0:T(8,128)(2,1)}, bf16[2048,128]{1,0:T(8,128)(2,1)}, f32[64,64]{1,0:T(8,128)}) custom-call(bf16[2048,128]{1,0:T(8,128)(2,1)S(1)} %get-tuple-element.6.a_ref, bf16[2048,128]{1,0:T(8,128)(2,1)S(1)} %get-tuple-element.7.b_ref, f32[64,64]{1,0:T(8,128)S(1)} %get-tuple-element.8.c_ref), custom_call_target="tpu_custom_call" | custom-call | tf_op jit(solution)/shard_map/pallas_call | solution.py:857
Async XLA Ops:
  0.6 0.8 %copy-start = (f32[64,64]{1,0:T(8,128)S(1)}, f32[64,64]{1,0:T(8,128)}, u32[]{:S(2)}) copy-start(f32[64,64]{1,0:T(8,128)} %raw_hbm.1) | copy-start | bytes 49156
